TPU v7x, 32 devices: a whole 2x2x4 slice. The times are simulated.
32 devices in a mesh: language: 2 (over core), fsdp: 16 (over z, y, x).
Axes of the slice: x: 2, y: 2, z: 4, core: 2. Of those that a mesh axis runs over, the one named last changes fastest.
Arguments:
- hidden: bfloat16 [4, 2048, 5120], P('language', 'fsdp'), may hold values from -60 to 60
- latent_grad: bfloat16 [4, 2048, 64], P('language', 'fsdp'), may hold values from -0.3125 to 0.3125
- lang_ids: int32 [4], P('language'), may hold values from 0 to 3, each once
- old_weights: float32 [4], replicated, may hold values from 0.02 to 0.2
- param: float32 [5120, 64], P('fsdp'), may hold values from -6 to 6
- first_moment: float32 [5120, 64], P('fsdp'), may hold values from -6 to 6
- second_moment: float32 [5120, 64], P('fsdp'), may hold values from 0.25 to 4
Outputs:
- new_param: float32 [5120, 64], P('fsdp')
- new_first: float32 [5120, 64], P('fsdp')
- new_second: float32 [5120, 64], P('fsdp')
- new_logweights: float32 [4], replicated
Inputs may be any that keep to these rules, and one draw needn't show every extreme that they name: `lang_ids`: each id appears in exactly one slot.
All inputs are finite; a program needn't handle non-finite values.
Results may differ from a plain program's by a relative error of at most 0.0003.
Values may be sent and summed in bfloat16 or wider, within the bound.
No kernel may reach another device: no remote copies, remote signals or barrier semaphores. Data moves between devices by JAX's collectives and lax.ppermute only.
A program may use at most 64 MiB of HBM per device.

v0:
```python
import jax
import jax.numpy as jnp
from jax import lax
from jax.sharding import PartitionSpec as P

STEP = 100


def log_weights(by_lang, square, old_weights):
    logits = jnp.log(old_weights) + old_weights.shape[0] * (by_lang / (square + 1e-06))
    return logits - jnp.log(jnp.sum(jnp.exp(logits)))


def local(hidden, latent_grad, lang_ids, old_weights, param, first_moment, second_moment):
    langs = old_weights.shape[0]
    slot_grad = lax.psum_scatter(
        jnp.einsum("ltd,ltr->dlr", hidden, latent_grad, preferred_element_type=jnp.float32),
        "fsdp",
        scatter_dimension=0,
        tiled=True,
    )
    onehot = (lang_ids[:, None] == jnp.arange(langs, dtype=jnp.int32)[None, :]).astype(jnp.float32)
    every_grad, every_hot = (
        lax.all_gather(slot_grad, "language", axis=1, tiled=True),
        lax.all_gather(onehot[None], "language", axis=1, tiled=True),
    )
    table = every_hot[0]
    total = jnp.sum(every_grad, axis=1)
    dots_part = jnp.einsum("dlr,dr->l", every_grad, total, precision=lax.Precision.HIGHEST)
    square_part = jnp.sum(total * total)
    dots, square = lax.psum((dots_part, square_part), "fsdp")
    by_lang = jnp.dot(dots, table, precision=lax.Precision.HIGHEST)
    new_logweights = log_weights(by_lang, square, old_weights)
    weights = jnp.exp(new_logweights)
    slot_weight = jnp.dot(table, weights, precision=lax.Precision.HIGHEST)
    update = jnp.einsum("l,dlr->dr", slot_weight, every_grad, precision=lax.Precision.HIGHEST)
    new_first = 0.9 * first_moment + 0.1 * update
    new_second = 0.95 * second_moment + 0.05 * update * update
    first_hat = new_first / (1.0 - 0.9**STEP)
    second_hat = new_second / (1.0 - 0.95**STEP)
    new_param = param - 0.02 * (first_hat / (jnp.sqrt(second_hat) + 1e-08) + 0.1 * param)
    return (new_param, new_first, new_second, new_logweights)


def solution(mesh):
    placed = (
        P("language", "fsdp", None),
        P("language", "fsdp", None),
        P("language"),
        P(),
        P("fsdp", None),
        P("fsdp", None),
        P("fsdp", None),
    )
    return jax.shard_map(
        local,
        mesh=mesh,
        in_specs=placed,
        out_specs=(P("fsdp", None), P("fsdp", None), P("fsdp", None), P()),
        check_vma=False,
    )
```

profile of v0, /device:TPU:0, one launch (start us, length us, event | category | flops | bytes accessed | tf_op | source)
XLA Modules:
  0.0 182.2 jit_solution(8020374576163812956)
XLA Ops:
  7.2 0.0 copy-start
  7.2 0.0 reduce-scatter.4.cloned.1.call-start
  7.2 1.7 copy-done
  8.9 2.8 %fusion.14 = f32[2,64,5120]{2,1,0:T(8,128)} fusion(bf16[2,128,64]{1,2,0:T(8,128)(2,1)} %param.8, bf16[2,128,5120]{2,1,0:T(8,128)(2,1)S(1)} %copy-done), kind=kOutput, calls=%fused_computation.22 | convolution fusion | flops 167772160 | bytes 5275648 | tf_op jit(solution)/shard_map/ltd,ltr->dlr/dot_general | solution.py:17
  11.7 3.2 %copy.16 = f32[5120,128]{1,0:T(8,128)} copy(f32[5120,128]{0,1:T(8,128)} %bitcast.41) | data formatting | bytes 5242880
  14.9 0.0 reduce-scatter.4.cloned.1.call-update
  14.9 0.6 copy-done.4
  15.6 0.1 compare_convert_fusion
  15.6 84.7 %reduce-scatter.4.cloned.1.call-done = f32[320,128]{1,0:T(8,128)} async-done(((f32[5120,128]{1,0:T(8,128)}), f32[320,128]{1,0:T(8,128)}) %reduce-scatter.4.cloned.1.call-update) | async-done | bytes 163856
  100.3 1.0 copy.17
  101.4 2.1 %all_gather.7 = f32[320,4,64]{0,2,1:T(8,128)S(1)} all-gather(f32[320,2,64]{0,2,1:T(8,128)S(1)} %bitcast.42), channel_id=1, replica_groups=mesh['language'=2,'fsdp'=16] {'language'}, dimensions={1}, use_global_device_ids=true | all-gather | bytes 491520 | tf_op jit(solution)/shard_map/all_gather | solution.py:24
  103.5 1.9 %convolution_bitcast_fusion.2 = f32[4]{0:T(128)S(1)} fusion(f32[320,4,64]{0,2,1:T(8,128)S(1)} %all_gather.7, f32[320,64,1]{0,1,2:T(8,128)S(1)} %bitcast.43), kind=kOutput, calls=%fused_computation.2 | convolution fusion | flops 983040 | bytes 409616 | tf_op jit(solution)/shard_map/dlr,dr->l/dot_general | solution.py:29
  105.4 0.6 multiply_reduce_fusion
  106.1 1.8 all_gather.6
  107.8 38.8 %all-reduce = (f32[4]{0:T(128)S(1)}, f32[]{:T(128)}) all-reduce(f32[4]{0:T(128)S(1)} %convolution_bitcast_fusion.2, f32[]{:T(128)} %multiply_reduce_fusion), channel_id=1, replica_groups=mesh['language'=2,'fsdp'=16] {'fsdp'}, use_global_device_ids=true, to_apply=%region_2.0 | all-reduce | flops 5 | bytes 40 | tf_op jit(solution)/shard_map/psum | solution.py:31
  147.3 0.0 copy-done.5
  147.3 0.7 exponential_reduce_fusion
  148.7 0.0 copy-start.6
  148.8 0.1 convolution_bitcast_fusion
  148.9 19.2 %fusion.3 = f32[1,320,64]{0,1,2:T(8,128)} fusion(f32[4,1,1]{0,1,2:T(1,128)S(1)} %convolution_bitcast_fusion, f32[320,4,64]{0,2,1:T(8,128)S(1)} %all_gather.7), kind=kOutput, calls=%fused_computation.6 | convolution fusion | flops 983040 | bytes 409616 | tf_op jit(solution)/shard_map/l,dlr->dr/dot_general | solution.py:36
  168.1 0.0 copy-done.6
  168.1 6.5 %copy.13 = f32[1,320,64]{1,2,0:T(8,128)S(1)} copy(f32[1,320,64]{0,1,2:T(8,128)} %fusion.3) | data formatting | bytes 163840 | tf_op jit(solution)/shard_map/l,dlr->dr/dot_general | solution.py:36
  174.6 0.0 copy-done.3
  174.6 0.7 multiply_subtract_fusion
  (9 shorter events, 0.0 us)
Async XLA Ops:
  7.2 1.7 copy-start
  7.2 93.1 %reduce-scatter.4.cloned.1.call-start = ((), (), s32[]{:S(2)}) async-start(), calls=%async_computation.1 | async-start | bytes 2785280
  14.9 0.7 copy-start.4
  14.9 132.4 %copy-start.5 = (f32[4]{0:T(128)S(1)}, f32[4]{0:T(128)}, u32[]{:S(2)}) copy-start(f32[4]{0:T(128)} %param.10) | copy-start | bytes 52
  148.7 19.3 %copy-start.6 = (f32[4]{0:T(128)}, f32[4]{0:T(128)S(1)}, u32[]{:S(2)}) copy-start(f32[4]{0:T(128)S(1)} %broadcast_subtract_fusion) | copy-start | bytes 52
  168.1 6.5 %copy-start.1 = (f32[320,64]{0,1:T(8,128)S(1)}, f32[320,64]{0,1:T(8,128)}, u32[]{:S(2)}) copy-start(f32[320,64]{0,1:T(8,128)} %param.11) | copy-start | bytes 245764
  168.1 6.5 %copy-start.2 = (f32[320,64]{0,1:T(8,128)S(1)}, f32[320,64]{0,1:T(8,128)}, u32[]{:S(2)}) copy-start(f32[320,64]{0,1:T(8,128)} %param.12) | copy-start | bytes 245764
  168.1 6.5 %copy-start.3 = (f32[320,64]{0,1:T(8,128)S(1)}, f32[320,64]{0,1:T(8,128)}, u32[]{:S(2)}) copy-start(f32[320,64]{0,1:T(8,128)} %param.13) | copy-start | bytes 245764
Sparse Core Ops, SparseCore 0:
  15.1 85.2 reduce-scatter.3
where the time goes:
time: 183 us; the launch traced here: 182 us
  waiting for transfers between devices  84.7 us (46%)
  blocking collectives  42.7 us (23%)
  matrix products  24.8 us (14%)
  between operations  15.4 us (8%)
  local copies, waits for them, and re-layouts  13.1 us (7%)
    unnamed x2, waiting for transfers between devices  84.7 us
    psum x1, blocking collectives, local(): dots, square = lax.psum((dots_part, square_part), 'fsdp')  38.8 us
    dot_general x1, matrix products, local(): jnp.einsum('l,dlr->dr', slot_weight, every_grad, precision=lax.Precision....  19.2 us
    unnamed x16, local copies, waits for them, and re-layouts  6.61 us
    dot_general x1, local copies, waits for them, and re-layouts, local(): jnp.einsum('l,dlr->dr', slot_weight, every_grad, precision=lax.Precision....  6.49 us
  transfers between devices with their start and end apart: 1, of which 1 were waited for; matrix products, arithmetic and copies ran while one was open for 0% of the time, Pallas kernels for 0%

commit v1 on v0

v1 whole, which is shorter than its diff:
```python
import functools
import math

import jax
import jax.numpy as jnp
from jax import lax
from jax.experimental import pallas as pl
from jax.experimental.pallas import tpu as pltpu
from jax.sharding import PartitionSpec as P

STEP = 100
SUB = 8
LANES = 128
FINE = 32.0
TOP = 32766.0
VMEM_LIMIT = 24 * 1024 * 1024
BOTH = ("language", "fsdp")


def whole(memory=pltpu.VMEM):
    return pl.BlockSpec(memory_space=memory)


def params():
    return pltpu.CompilerParams(vmem_limit_bytes=VMEM_LIMIT)


def encode(block):
    rows, lanes = block.shape
    half = rows // 2
    top = jnp.max(jnp.abs(block).reshape(rows // SUB, SUB, lanes), axis=0)
    step = jnp.ceil(jnp.log2(jnp.maximum(top, 1e-30)) * FINE)
    scale = jnp.exp2(step * (-1.0 / FINE)) * TOP
    codes = block.reshape(rows // SUB, SUB, lanes) * scale[None] + 32768.5
    codes = codes.astype(jnp.int32).reshape(rows, lanes)
    words = lax.shift_left(codes[:half], 16) | codes[half:]
    return words, step.astype(jnp.int32)


def decode(words, step):
    half, lanes = words.shape
    scale = jnp.exp2(step.astype(jnp.float32) * (1.0 / FINE)) * (1.0 / TOP)
    high = lax.shift_right_logical(words, 16).astype(jnp.float32) - 32768.0
    low = (words & 65535).astype(jnp.float32) - 32768.0
    both = jnp.concatenate([high, low], axis=0).reshape(2 * half // SUB, SUB, lanes)
    return (both * scale[None]).reshape(2 * half, lanes)


def spot(me, parity, index, bits):
    p = jnp.bitwise_xor(me, index)
    swap = (p ^ (p >> 1)) & 1 & parity
    p = p ^ (swap | (swap << 1))
    out = jnp.int32(0)
    for k in range(bits):
        out = out | (((p >> k) & 1) << (bits - 1 - k))
    return out


def first_kernel(blocks, rows, where_ref, hidden_ref, latent_ref, keep_ref, send_ref):
    bits = blocks.bit_length() - 1
    slots, tokens, width = hidden_ref.shape
    rank = latent_ref.shape[1]
    zero = jnp.zeros((rank, tokens), latent_ref.dtype)
    left = jnp.concatenate(
        [jnp.concatenate([latent_ref[a] if a == b else zero for b in range(slots)], axis=1) for a in range(slots)], axis=0
    )
    grad = jnp.dot(left, hidden_ref[...].reshape(slots * tokens, width), preferred_element_type=jnp.float32).T
    per = width // rows
    for k in range(per):
        at = spot(where_ref[0], where_ref[1], pl.program_id(0) * per + k, bits)
        block = grad[k * rows : (k + 1) * rows]

        @pl.when(at < blocks // 2)
        def _():
            keep_ref[at] = block

        @pl.when(at >= blocks // 2)
        def _():
            words, step = encode(block)
            send_ref[at - blocks // 2, : rows // 2] = words
            send_ref[at - blocks // 2, rows // 2 :] = step


def first(hidden, latent, where, blocks):
    slots, tokens, dim = hidden.shape
    rows = dim // blocks
    width = math.lcm(rows, LANES)
    lanes = slots * latent.shape[1]
    return pl.pallas_call(
        functools.partial(first_kernel, blocks, rows),
        grid_spec=pltpu.PrefetchScalarGridSpec(
            num_scalar_prefetch=1,
            grid=(dim // width,),
            in_specs=[
                pl.BlockSpec((slots, tokens, width), lambda q, w: (0, 0, q)),
                pl.BlockSpec(latent.shape, lambda q, w: (0, 0, 0)),
            ],
            out_specs=[
                pl.BlockSpec((blocks // 2, rows, lanes), lambda q, w: (0, 0, 0)),
                pl.BlockSpec((blocks // 2, rows // 2 + SUB, lanes), lambda q, w: (0, 0, 0)),
            ],
        ),
        out_shape=[
            jax.ShapeDtypeStruct((blocks // 2, rows, lanes), jnp.float32),
            jax.ShapeDtypeStruct((blocks // 2, rows // 2 + SUB, lanes), jnp.int32),
        ],
        compiler_params=params(),
    )(where, hidden, latent)


def added(got_ref, keep_ref, at):
    half = got_ref.shape[1] - SUB
    return keep_ref[at] + decode(got_ref[at, :half], got_ref[at, half:])


def middle_kernel(got_ref, keep_ref, left_ref, send_ref):
    blocks = keep_ref.shape[0]
    half = keep_ref.shape[1] // 2
    for k in range(blocks // 2):
        words, step = encode(added(got_ref, keep_ref, blocks // 2 + k))
        send_ref[k, :half] = words
        send_ref[k, half:] = step
    for k in range(blocks // 2):
        left_ref[k] = added(got_ref, keep_ref, k)


def middle(got, keep):
    blocks, rows, lanes = keep.shape
    return pl.pallas_call(
        middle_kernel,
        in_specs=[whole(), whole()],
        out_specs=[whole(), whole()],
        out_shape=[
            jax.ShapeDtypeStruct((blocks // 2, rows, lanes), jnp.float32),
            jax.ShapeDtypeStruct((blocks // 2, rows // 2 + SUB, lanes), jnp.int32),
        ],
        compiler_params=params(),
    )(got, keep)


def last_kernel(ids_ref, got_ref, keep_ref, out_ref):
    rows, lanes = keep_ref.shape[1:]
    slots = ids_ref.shape[0]
    out_ref[:rows] = added(got_ref, keep_ref, 0)
    slot = lax.broadcasted_iota(jnp.int32, (SUB, lanes), 1) // (lanes // slots)
    row = jnp.zeros((SUB, lanes), jnp.float32)
    for s in range(slots):
        row = jnp.where(slot == s, ids_ref[s].astype(jnp.float32), row)
    out_ref[rows:] = row


def last(ids, got, keep):
    _, rows, lanes = keep.shape
    return pl.pallas_call(
        last_kernel,
        in_specs=[whole(pltpu.SMEM), whole(), whole()],
        out_specs=whole(),
        out_shape=jax.ShapeDtypeStruct((rows + SUB, lanes), jnp.float32),
        compiler_params=params(),
    )(ids, got, keep)


def spread(x, rank):
    lanes = x.shape[1]
    out = x
    shift = rank
    while shift < lanes:
        out = out + pltpu.roll(out, shift, 1)
        shift *= 2
    return out


def dots_kernel(rank, every_ref, out_ref):
    groups, rows, lanes = every_ref.shape
    rows -= SUB
    total = every_ref[0, :rows]
    for g in range(1, groups):
        total = total + every_ref[g, :rows]
    total = spread(total, rank)
    out_ref[...] = jnp.zeros_like(out_ref)
    for g in range(groups):
        out_ref[g : g + 1] = jnp.sum(every_ref[g, :rows] * total, axis=0, keepdims=True)
    out_ref[groups : groups + 1] = jnp.sum(total * total, axis=0, keepdims=True)


def dots(every, rank):
    groups, _, lanes = every.shape
    return pl.pallas_call(
        functools.partial(dots_kernel, rank),
        in_specs=[whole()],
        out_specs=whole(),
        out_shape=jax.ShapeDtypeStruct((pl.cdiv(groups + 1, SUB) * SUB, lanes), jnp.float32),
        compiler_params=params(),
    )(every)


def turn_kernel(every_ref, out_ref):
    groups, rows, _ = every_ref.shape
    for g in range(groups):
        out_ref[g] = every_ref[g, : rows - SUB].T


def turn(every):
    groups, rows, lanes = every.shape
    return pl.pallas_call(
        turn_kernel,
        in_specs=[whole()],
        out_specs=whole(),
        out_shape=jax.ShapeDtypeStruct((groups, lanes, rows - SUB), jnp.float32),
        compiler_params=params(),
    )(every)


def final_kernel(
    sums_ref, every_ref, grad_ref, old_ref, param_ref, first_ref, second_ref, new_param_ref, new_first_ref, new_second_ref, log_ref
):
    groups, lanes, _ = grad_ref.shape
    langs = old_ref.shape[1]
    rank = param_ref.shape[0]
    slots = lanes // rank
    parts = sums_ref[:groups]
    square = jnp.sum(sums_ref[groups : groups + 1, :rank], axis=1, keepdims=True) + 1e-06
    ids = jnp.concatenate([every_ref[g, :1] for g in range(groups)], axis=0)
    at = lax.broadcasted_iota(jnp.int32, (1, langs), 1)
    align = jnp.zeros((1, langs), jnp.float32)
    for k in range(langs):
        one = jnp.sum(jnp.where(ids == float(k), parts, 0.0), axis=1, keepdims=True)
        align = jnp.where(at == k, jnp.sum(one, axis=0, keepdims=True), align)
    logits = jnp.log(old_ref[...]) + float(langs) * (align / square)
    logs = logits - jnp.log(jnp.sum(jnp.exp(logits), axis=1, keepdims=True))
    log_ref[...] = logs
    weights = jnp.exp(logs)
    update = None
    for g in range(groups):
        for s in range(slots):
            own = ids[g : g + 1, s * rank : s * rank + 1]
            weight = jnp.zeros((1, 1), jnp.float32)
            for k in range(langs):
                weight = weight + jnp.where(own == float(k), weights[:, k : k + 1], 0.0)
            term = weight * grad_ref[g, s * rank : (s + 1) * rank]
            update = term if update is None else update + term
    new_first = 0.9 * first_ref[...] + 0.1 * update
    new_second = 0.95 * second_ref[...] + 0.05 * update * update
    first_hat = new_first / (1.0 - 0.9**STEP)
    second_hat = new_second / (1.0 - 0.95**STEP)
    param = param_ref[...]
    new_param_ref[...] = param - 0.02 * (first_hat / (jnp.sqrt(second_hat) + 1e-08) + 0.1 * param)
    new_first_ref[...] = new_first
    new_second_ref[...] = new_second


def final(sums, every, grads, old, param, first_moment, second_moment):
    groups, rows, lanes = every.shape
    shape = jax.ShapeDtypeStruct(param.shape, jnp.float32)
    whole_of = lambda x: pl.BlockSpec(x.shape, lambda i: (0,) * len(x.shape))
    return pl.pallas_call(
        final_kernel,
        grid=(1,),
        in_specs=[
            whole_of(sums),
            pl.BlockSpec((groups, SUB, lanes), lambda i: (0, rows // SUB - 1, 0)),
            whole_of(grads),
            whole_of(old),
            whole_of(param),
            whole_of(param),
            whole_of(param),
        ],
        out_specs=[whole_of(param), whole_of(param), whole_of(param), whole_of(old)],
        out_shape=[shape, shape, shape, jax.ShapeDtypeStruct(old.shape, jnp.float32)],
        compiler_params=params(),
    )(sums, every, grads, old, param, first_moment, second_moment)


def local(groups, blocks, hidden, latent_grad, lang_ids, old_weights, param, first_moment, second_moment):
    bits = blocks.bit_length() - 1
    rank = latent_grad.shape[2]

    def flip(even, odd):
        pairs = [(g * blocks + f, g * blocks + (f ^ (1 << (odd if g % 2 else even)))) for g in range(groups) for f in range(blocks)]
        return functools.partial(lax.ppermute, axis_name=BOTH, perm=pairs)

    where = jnp.stack([lax.axis_index("fsdp"), lax.axis_index("language") % 2]).astype(jnp.int32)
    keep, send = first(hidden, latent_grad.transpose(0, 2, 1), where, blocks)
    for k in range(bits):
        got = flip(k, 1 - k if k < 2 else k)(send)
        if k < bits - 1:
            keep, send = middle(got, keep)
    mine = last(lang_ids, got, keep)
    every = lax.all_gather(mine, "language")
    sums = dots(every, rank)
    grads = turn(every)
    for k in range(bits):
        sums = sums + flip(k, k)(sums)
    new_param, new_first, new_second, logs = final(
        sums, every, grads, old_weights[None], param.T, first_moment.T, second_moment.T
    )
    return new_param.T, new_first.T, new_second.T, logs[0]


def solution(mesh):
    placed = (
        P("language", "fsdp", None),
        P("language", "fsdp", None),
        P("language"),
        P(),
        P("fsdp", None),
        P("fsdp", None),
        P("fsdp", None),
    )
    return jax.shard_map(
        functools.partial(local, mesh.shape["language"], mesh.shape["fsdp"]),
        mesh=mesh,
        in_specs=placed,
        out_specs=(P("fsdp", None), P("fsdp", None), P("fsdp", None), P()),
        check_vma=False,
    )
```

time: 183 us -> 58.6 us (0.32)
  waiting for transfers between devices: 84.7 us -> 27.3 us
  blocking collectives: 42.7 us -> 2.05 us
  matrix products: 24.8 us -> 0 us
  starting transfers between devices: 0.04 us -> 18.8 us
  between operations: 15.4 us -> 0.72 us
  local copies, waits for them, and re-layouts: 13.1 us -> 2.52 us
  Pallas kernels: 0 us -> 6.89 us
    unnamed x2 -> x0, waiting for transfers between devices: 84.7 us -> none
    psum x1 -> x0, blocking collectives: 38.8 us -> none  [local(): dots, square = lax.psum((dots_part, square_part), 'fsdp')]
    ppermute x0 -> x8, waiting for transfers between devices: none -> 27.3 us  [the longest x4 20.2 us: local(): got = flip(k, 1 - k if k < 2 else k)(send)]
    dot_general x5 -> x0, matrix products: 24.8 us -> none  [the longest x1 19.2 us: local(): jnp.einsum('l,dlr->dr', slot_weight, every_grad, precision=lax.Precision....]
    ppermute x0 -> x8, starting transfers between devices: none -> 18.8 us  [the longest x4 10.5 us: local(): got = flip(k, 1 - k if k < 2 else k)(send)]
    pallas_call x0 -> x8, Pallas kernels: none -> 6.89 us  [the longest x1 4.17 us: first(): pl.pallas_call(functools.partial(first_kernel, blocks, rows), grid_spec=p...]
    dot_general x1 -> x0, local copies, waits for them, and re-layouts: 6.49 us -> none  [local(): jnp.einsum('l,dlr->dr', slot_weight, every_grad, precision=lax.Precision....]
    unnamed x16 -> x14, local copies, waits for them, and re-layouts: 6.61 us -> 2.52 us
  transfers between devices with their start and end apart: 1 -> 8, of which waited for: 1 -> 8; matrix products, arithmetic and copies ran while one was open for 0% -> 0% of each run, Pallas kernels for 0% -> 0%
where the time goes in v1:
time: 58.6 us; the launch traced here: 58.3 us
  waiting for transfers between devices  27.3 us (47%)
  starting transfers between devices  18.8 us (32%)
  Pallas kernels  6.89 us (12%)
  local copies, waits for them, and re-layouts  2.52 us (4%)
  blocking collectives  2.05 us (3%)
  between operations  0.72 us (1%)
    ppermute x4, waiting for transfers between devices, local(): got = flip(k, 1 - k if k < 2 else k)(send)  20.2 us
    ppermute x4, starting transfers between devices, local(): got = flip(k, 1 - k if k < 2 else k)(send)  10.5 us
    ppermute x4, starting transfers between devices, local(): sums = sums + flip(k, k)(sums)  8.31 us
    ppermute x4, waiting for transfers between devices, local(): sums = sums + flip(k, k)(sums)  7.1 us
    pallas_call x1, Pallas kernels, first(): pl.pallas_call(functools.partial(first_kernel, blocks, rows), grid_spec=p...  4.17 us
    unnamed x14, local copies, waits for them, and re-layouts  2.52 us
    all_gather x1, blocking collectives, local(): every = lax.all_gather(mine, 'language')  2.05 us
  transfers between devices with their start and end apart: 8, of which 8 were waited for; matrix products, arithmetic and copies ran while one was open for 0% of the time, Pallas kernels for 0%

profile of v1, /device:TPU:0, one launch (start us, length us, event | category | flops | bytes accessed | tf_op | source)
XLA Modules:
  0.0 58.3 jit_solution(2779216458062424040)
XLA Ops:
  0.7 1.7 %copy-done = bf16[2,128,5120]{2,1,0:T(8,128)(2,1)S(1)} copy-done((bf16[2,128,5120]{2,1,0:T(8,128)(2,1)S(1)}, bf16[2,128,5120]{2,1,0:T(8,128)(2,1)}, u32[]{:S(2)}) %copy-start) | copy-done | bytes 2621464
  2.5 0.8 %copy-done.4 = bf16[2,128,64]{1,2,0:T(8,128)(2,1)S(1)} copy-done((bf16[2,128,64]{1,2,0:T(8,128)(2,1)S(1)}, bf16[2,128,64]{1,2,0:T(8,128)(2,1)}, u32[]{:S(2)}) %copy-start.4) | copy-done | bytes 32792
  3.2 4.2 %shard_map.102 = (f32[8,320,128]{2,1,0:T(8,128)S(1)}, s32[8,168,128]{2,1,0:T(8,128)S(1)}) custom-call(s32[2]{0:T(128)S(1)} %pad_add_fusion.where_ref, bf16[2,128,5120]{2,1,0:T(8,128)(2,1)S(1)} %copy-done, bf16[2,64,128]{2,1,0:T(8,128)(2,1)S(1)} %bitcast.18), custom_call_target="tpu_custom_call" | custom-call | tf_op jit(solution)/shard_map/pallas_call | solution.py:89
  7.4 3.2 %collective-permute-start = (s32[8,168,128]{2,1,0:T(8,128)S(1)}, s32[8,168,128]{2,1,0:T(8,128)S(1)}, u32[]{:S(2)}, u32[]{:S(2)}) collective-permute-start(s32[8,168,128]{2,1,0:T(8,128)S(1)} %get-tuple-element.16), channel_id=1, source_target_pairs={{0,1},{1,0},{2,3},{3,2},{4,5},{5,4},{6,7},{7,6},{8,9},{9,8},{10,11... | collective-permute-start | bytes 2064392 | tf_op jit(solution)/shard_map/ppermute | solution.py:285
  10.6 8.9 %collective-permute-done.got_ref = s32[8,168,128]{2,1,0:T(8,128)S(1)} collective-permute-done((s32[8,168,128]{2,1,0:T(8,128)S(1)}, s32[8,168,128]{2,1,0:T(8,128)S(1)}, u32[]{:S(2)}, u32[]{:S(2)}) %collective-permute-start) | collective-permute-done | bytes 688160 | tf_op jit(solution)/shard_map/ppermute | solution.py:285
  19.5 0.4 shard_map.103
  19.9 2.0 %collective-permute-start.1 = (s32[4,168,128]{2,1,0:T(8,128)S(1)}, s32[4,168,128]{2,1,0:T(8,128)S(1)}, u32[]{:S(2)}, u32[]{:S(2)}) collective-permute-start(s32[4,168,128]{2,1,0:T(8,128)S(1)} %get-tuple-element.18), channel_id=1, source_target_pairs={{0,2},{1,3},{2,0},{3,1},{4,6},{5,7},{6,4},{7,5},{8,10},{9,11},{10,... | collective-permute-start | bytes 1032200 | tf_op jit(solution)/shard_map/ppermute | solution.py:285
  21.9 5.4 %collective-permute-done.1.got_ref = s32[4,168,128]{2,1,0:T(8,128)S(1)} collective-permute-done((s32[4,168,128]{2,1,0:T(8,128)S(1)}, s32[4,168,128]{2,1,0:T(8,128)S(1)}, u32[]{:S(2)}, u32[]{:S(2)}) %collective-permute-start.1) | collective-permute-done | bytes 344096 | tf_op jit(solution)/shard_map/ppermute | solution.py:285
  27.2 0.2 shard_map.104
  27.4 2.0 %collective-permute-start.2 = (s32[2,168,128]{2,1,0:T(8,128)S(1)}, s32[2,168,128]{2,1,0:T(8,128)S(1)}, u32[]{:S(2)}, u32[]{:S(2)}) collective-permute-start(s32[2,168,128]{2,1,0:T(8,128)S(1)} %get-tuple-element.20), channel_id=1, source_target_pairs={{0,4},{1,5},{2,6},{3,7},{4,0},{5,1},{6,2},{7,3},{8,12},{9,13},{10,... | collective-permute-start | bytes 516104 | tf_op jit(solution)/shard_map/ppermute | solution.py:285
  29.5 3.5 %collective-permute-done.2.got_ref = s32[2,168,128]{2,1,0:T(8,128)S(1)} collective-permute-done((s32[2,168,128]{2,1,0:T(8,128)S(1)}, s32[2,168,128]{2,1,0:T(8,128)S(1)}, u32[]{:S(2)}, u32[]{:S(2)}) %collective-permute-start.2) | collective-permute-done | bytes 172064 | tf_op jit(solution)/shard_map/ppermute | solution.py:285
  33.0 3.3 %collective-permute-start.3 = (s32[1,168,128]{2,1,0:T(8,128)S(1)}, s32[1,168,128]{2,1,0:T(8,128)S(1)}, u32[]{:S(2)}, u32[]{:S(2)}) collective-permute-start(s32[1,168,128]{2,1,0:T(8,128)S(1)} %get-tuple-element.22), channel_id=1, source_target_pairs={{0,8},{1,9},{2,10},{3,11},{4,12},{5,13},{6,14},{7,15},{8,0},{9,1},... | collective-permute-start | bytes 258056 | tf_op jit(solution)/shard_map/ppermute | solution.py:285
  36.3 2.5 %collective-permute-done.3.got_ref = s32[1,168,128]{2,1,0:T(8,128)S(1)} collective-permute-done((s32[1,168,128]{2,1,0:T(8,128)S(1)}, s32[1,168,128]{2,1,0:T(8,128)S(1)}, u32[]{:S(2)}, u32[]{:S(2)}) %collective-permute-start.3) | collective-permute-done | bytes 86048 | tf_op jit(solution)/shard_map/ppermute | solution.py:285
  38.8 0.6 shard_map.106
  39.4 2.0 %all-gather = f32[656,128]{1,0:T(8,128)S(1)} all-gather(f32[328,128]{1,0:T(8,128)S(1)} %shard_map.106), channel_id=2, replica_groups=mesh['language'=2,'fsdp'=16] {'language'}, dimensions={0}, use_global_device_ids=true | all-gather | bytes 503808 | tf_op jit(solution)/shard_map/all_gather | solution.py:289
  41.6 1.9 %collective-permute-start.4 = (f32[8,128]{1,0:T(8,128)S(1)}, f32[8,128]{1,0:T(8,128)S(1)}, u32[]{:S(2)}, u32[]{:S(2)}) collective-permute-start(f32[8,128]{1,0:T(8,128)S(1)} %shard_map.107), channel_id=1, source_target_pairs={{0,1},{1,0},{2,3},{3,2},{4,5},{5,4},{6,7},{7,6},{8,9},{9,8},{10,11... | collective-permute-start | bytes 12296 | tf_op jit(solution)/shard_map/ppermute | solution.py:293
  43.4 1.8 %collective-permute-done.4 = f32[8,128]{1,0:T(8,128)S(1)} collective-permute-done((f32[8,128]{1,0:T(8,128)S(1)}, f32[8,128]{1,0:T(8,128)S(1)}, u32[]{:S(2)}, u32[]{:S(2)}) %collective-permute-start.4) | collective-permute-done | bytes 4128 | tf_op jit(solution)/shard_map/ppermute | solution.py:293
  45.2 1.6 %collective-permute-start.5 = (f32[8,128]{1,0:T(8,128)S(1)}, f32[8,128]{1,0:T(8,128)S(1)}, u32[]{:S(2)}, u32[]{:S(2)}) collective-permute-start(f32[8,128]{1,0:T(8,128)S(1)} %add.17), channel_id=1, source_target_pairs={{0,2},{1,3},{2,0},{3,1},{4,6},{5,7},{6,4},{7,5},{8,10},{9,11},{10,... | collective-permute-start | bytes 12296 | tf_op jit(solution)/shard_map/ppermute | solution.py:293
  46.8 2.0 %collective-permute-done.5 = f32[8,128]{1,0:T(8,128)S(1)} collective-permute-done((f32[8,128]{1,0:T(8,128)S(1)}, f32[8,128]{1,0:T(8,128)S(1)}, u32[]{:S(2)}, u32[]{:S(2)}) %collective-permute-start.5) | collective-permute-done | bytes 4128 | tf_op jit(solution)/shard_map/ppermute | solution.py:293
  48.9 1.8 %collective-permute-start.6 = (f32[8,128]{1,0:T(8,128)S(1)}, f32[8,128]{1,0:T(8,128)S(1)}, u32[]{:S(2)}, u32[]{:S(2)}) collective-permute-start(f32[8,128]{1,0:T(8,128)S(1)} %add.18), channel_id=1, source_target_pairs={{0,4},{1,5},{2,6},{3,7},{4,0},{5,1},{6,2},{7,3},{8,12},{9,13},{10,... | collective-permute-start | bytes 12296 | tf_op jit(solution)/shard_map/ppermute | solution.py:293
  50.6 1.9 %collective-permute-done.6 = f32[8,128]{1,0:T(8,128)S(1)} collective-permute-done((f32[8,128]{1,0:T(8,128)S(1)}, f32[8,128]{1,0:T(8,128)S(1)}, u32[]{:S(2)}, u32[]{:S(2)}) %collective-permute-start.6) | collective-permute-done | bytes 4128 | tf_op jit(solution)/shard_map/ppermute | solution.py:293
  52.5 3.1 %collective-permute-start.7 = (f32[8,128]{1,0:T(8,128)S(1)}, f32[8,128]{1,0:T(8,128)S(1)}, u32[]{:S(2)}, u32[]{:S(2)}) collective-permute-start(f32[8,128]{1,0:T(8,128)S(1)} %add.19), channel_id=1, source_target_pairs={{0,8},{1,9},{2,10},{3,11},{4,12},{5,13},{6,14},{7,15},{8,0},{9,1},... | collective-permute-start | bytes 12296 | tf_op jit(solution)/shard_map/ppermute | solution.py:293
  55.7 1.4 %collective-permute-done.7 = f32[8,128]{1,0:T(8,128)S(1)} collective-permute-done((f32[8,128]{1,0:T(8,128)S(1)}, f32[8,128]{1,0:T(8,128)S(1)}, u32[]{:S(2)}, u32[]{:S(2)}) %collective-permute-start.7) | collective-permute-done | bytes 4128 | tf_op jit(solution)/shard_map/ppermute | solution.py:293
  57.2 1.1 %shard_map.109 = (f32[64,320]{1,0:T(8,128)}, f32[64,320]{1,0:T(8,128)}, f32[64,320]{1,0:T(8,128)}, f32[1,4]{1,0:T(1,128)}) custom-call(f32[8,128]{1,0:T(8,128)S(1)} %add.20.sums_ref, f32[2,328,128]{2,1,0:T(8,128)S(1)} %bitcast.14, f32[2,128,320]{2,1,0:T(8,128)S(1)} %shard_map.108.grad_ref, f32[1,4]{1,0:T(1,128)S(1)} %bitcast.19, f32[64,320]{1,0:T(8,128)S(1)} %bitcast.15, ...), custom_call_target="tpu_custom_call" | custom-call | tf_op jit(solution)/shard_map/pallas_call | solution.py:256
  (20 shorter events, 0.5 us)
Async XLA Ops:
  0.7 1.7 %copy-start = (bf16[2,128,5120]{2,1,0:T(8,128)(2,1)S(1)}, bf16[2,128,5120]{2,1,0:T(8,128)(2,1)}, u32[]{:S(2)}) copy-start(bf16[2,128,5120]{2,1,0:T(8,128)(2,1)} %hidden_ref.1) | copy-start | bytes 7864324
  2.5 0.8 %copy-start.4 = (bf16[2,128,64]{1,2,0:T(8,128)(2,1)S(1)}, bf16[2,128,64]{1,2,0:T(8,128)(2,1)}, u32[]{:S(2)}) copy-start(bf16[2,128,64]{1,2,0:T(8,128)(2,1)} %param.8) | copy-start | bytes 98308
  3.2 35.6 %copy-start.6 = (s32[2]{0:T(128)S(1)}, s32[2]{0:T(128)}, u32[]{:S(2)}) copy-start(s32[2]{0:T(128)} %ids_ref.1) | copy-start | bytes 28
  7.4 12.1 %collective-permute-start = (s32[8,168,128]{2,1,0:T(8,128)S(1)}, s32[8,168,128]{2,1,0:T(8,128)S(1)}, u32[]{:S(2)}, u32[]{:S(2)}) collective-permute-start(s32[8,168,128]{2,1,0:T(8,128)S(1)} %get-tuple-element.16), channel_id=1, source_target_pairs={{0,1},{1,0},{2,3},{3,2},{4,5},{5,4},{6,7},{7,6},{8,9},{9,8},{10,11... | collective-permute-start | bytes 2064392 | tf_op jit(solution)/shard_map/ppermute | solution.py:285
  19.5 37.7 %copy-start.1 = (f32[320,64]{0,1:T(8,128)S(1)}, f32[320,64]{0,1:T(8,128)}, u32[]{:S(2)}) copy-start(f32[320,64]{0,1:T(8,128)} %param.11) | copy-start | bytes 245764
  19.5 37.7 %copy-start.2 = (f32[320,64]{0,1:T(8,128)S(1)}, f32[320,64]{0,1:T(8,128)}, u32[]{:S(2)}) copy-start(f32[320,64]{0,1:T(8,128)} %param.12) | copy-start | bytes 245764
  19.5 37.7 %copy-start.3 = (f32[320,64]{0,1:T(8,128)S(1)}, f32[320,64]{0,1:T(8,128)}, u32[]{:S(2)}) copy-start(f32[320,64]{0,1:T(8,128)} %param.13) | copy-start | bytes 245764
  19.5 37.7 %copy-start.5 = (f32[4]{0:T(128)S(1)}, f32[4]{0:T(128)}, u32[]{:S(2)}) copy-start(f32[4]{0:T(128)} %param.10) | copy-start | bytes 52
  19.9 7.3 %collective-permute-start.1 = (s32[4,168,128]{2,1,0:T(8,128)S(1)}, s32[4,168,128]{2,1,0:T(8,128)S(1)}, u32[]{:S(2)}, u32[]{:S(2)}) collective-permute-start(s32[4,168,128]{2,1,0:T(8,128)S(1)} %get-tuple-element.18), channel_id=1, source_target_pairs={{0,2},{1,3},{2,0},{3,1},{4,6},{5,7},{6,4},{7,5},{8,10},{9,11},{10,... | collective-permute-start | bytes 1032200 | tf_op jit(solution)/shard_map/ppermute | solution.py:285
  27.4 5.5 %collective-permute-start.2 = (s32[2,168,128]{2,1,0:T(8,128)S(1)}, s32[2,168,128]{2,1,0:T(8,128)S(1)}, u32[]{:S(2)}, u32[]{:S(2)}) collective-permute-start(s32[2,168,128]{2,1,0:T(8,128)S(1)} %get-tuple-element.20), channel_id=1, source_target_pairs={{0,4},{1,5},{2,6},{3,7},{4,0},{5,1},{6,2},{7,3},{8,12},{9,13},{10,... | collective-permute-start | bytes 516104 | tf_op jit(solution)/shard_map/ppermute | solution.py:285
  33.0 5.8 %collective-permute-start.3 = (s32[1,168,128]{2,1,0:T(8,128)S(1)}, s32[1,168,128]{2,1,0:T(8,128)S(1)}, u32[]{:S(2)}, u32[]{:S(2)}) collective-permute-start(s32[1,168,128]{2,1,0:T(8,128)S(1)} %get-tuple-element.22), channel_id=1, source_target_pairs={{0,8},{1,9},{2,10},{3,11},{4,12},{5,13},{6,14},{7,15},{8,0},{9,1},... | collective-permute-start | bytes 258056 | tf_op jit(solution)/shard_map/ppermute | solution.py:285
  41.6 3.7 %collective-permute-start.4 = (f32[8,128]{1,0:T(8,128)S(1)}, f32[8,128]{1,0:T(8,128)S(1)}, u32[]{:S(2)}, u32[]{:S(2)}) collective-permute-start(f32[8,128]{1,0:T(8,128)S(1)} %shard_map.107), channel_id=1, source_target_pairs={{0,1},{1,0},{2,3},{3,2},{4,5},{5,4},{6,7},{7,6},{8,9},{9,8},{10,11... | collective-permute-start | bytes 12296 | tf_op jit(solution)/shard_map/ppermute | solution.py:293
  45.2 3.6 %collective-permute-start.5 = (f32[8,128]{1,0:T(8,128)S(1)}, f32[8,128]{1,0:T(8,128)S(1)}, u32[]{:S(2)}, u32[]{:S(2)}) collective-permute-start(f32[8,128]{1,0:T(8,128)S(1)} %add.17), channel_id=1, source_target_pairs={{0,2},{1,3},{2,0},{3,1},{4,6},{5,7},{6,4},{7,5},{8,10},{9,11},{10,... | collective-permute-start | bytes 12296 | tf_op jit(solution)/shard_map/ppermute | solution.py:293
  48.9 3.6 %collective-permute-start.6 = (f32[8,128]{1,0:T(8,128)S(1)}, f32[8,128]{1,0:T(8,128)S(1)}, u32[]{:S(2)}, u32[]{:S(2)}) collective-permute-start(f32[8,128]{1,0:T(8,128)S(1)} %add.18), channel_id=1, source_target_pairs={{0,4},{1,5},{2,6},{3,7},{4,0},{5,1},{6,2},{7,3},{8,12},{9,13},{10,... | collective-permute-start | bytes 12296 | tf_op jit(solution)/shard_map/ppermute | solution.py:293
  52.5 4.7 %collective-permute-start.7 = (f32[8,128]{1,0:T(8,128)S(1)}, f32[8,128]{1,0:T(8,128)S(1)}, u32[]{:S(2)}, u32[]{:S(2)}) collective-permute-start(f32[8,128]{1,0:T(8,128)S(1)} %add.19), channel_id=1, source_target_pairs={{0,8},{1,9},{2,10},{3,11},{4,12},{5,13},{6,14},{7,15},{8,0},{9,1},... | collective-permute-start | bytes 12296 | tf_op jit(solution)/shard_map/ppermute | solution.py:293

commit v2 on v1

--- a/solution.py
+++ b/solution.py
@@ -46,66 +46,78 @@
     return (both * scale[None]).reshape(2 * half, lanes)
 
 
-def spot(me, parity, index, bits):
-    p = jnp.bitwise_xor(me, index)
-    swap = (p ^ (p >> 1)) & 1 & parity
-    p = p ^ (swap | (swap << 1))
-    out = jnp.int32(0)
-    for k in range(bits):
-        out = out | (((p >> k) & 1) << (bits - 1 - k))
-    return out
-
-
-def first_kernel(blocks, rows, where_ref, hidden_ref, latent_ref, keep_ref, send_ref):
+def place(blocks, parity, chain, half, index):
     bits = blocks.bit_length() - 1
-    slots, tokens, width = hidden_ref.shape
-    rank = latent_ref.shape[1]
-    zero = jnp.zeros((rank, tokens), latent_ref.dtype)
+    p = (half << parity) | (chain << (bits - 1))
+    for k in range(1, bits - 1):
+        bit = (index >> (bits - 2 - k)) & 1
+        p |= bit << (1 - parity if k == 1 else k)
+    return p
+
+
+def grad_kernel(blocks, parts, coded, hidden_ref, latent_ref, *refs):
+    out_refs, (hidden, latent, turned, sems) = refs[: len(parts)], refs[len(parts) :]
+    count, slots, tokens, width = hidden.shape
+    rank = latent.shape[1]
+    rows = hidden_ref.shape[2] // blocks
+    per = blocks // 4
+    me, parity = lax.axis_index("fsdp"), lax.axis_index("language") % 2
+    starts = []
+    for chain, half in parts:
+        for k in range(per):
+            even, odd = place(blocks, 0, chain, half, k), place(blocks, 1, chain, half, k)
+            starts.append(jnp.bitwise_xor(me, jnp.where(parity == 1, odd, even)) * rows)
+    small = pltpu.make_async_copy(latent_ref, latent, sems.at[count])
+    small.start()
+    copies, bases = [], []
+    for k in range(count):
+        base = jnp.minimum(starts[k] // LANES, (hidden_ref.shape[2] - width) // LANES) * LANES
+        bases.append(pl.multiple_of(base, LANES))
+        base = bases[k]
+        copies.append(pltpu.make_async_copy(hidden_ref.at[:, :, pl.ds(base, width)], hidden.at[k], sems.at[k]))
+        copies[k].start()
+    small.wait()
+    zero = jnp.zeros((rank, tokens), latent.dtype)
     left = jnp.concatenate(
-        [jnp.concatenate([latent_ref[a] if a == b else zero for b in range(slots)], axis=1) for a in range(slots)], axis=0
-    )
-    grad = jnp.dot(left, hidden_ref[...].reshape(slots * tokens, width), preferred_element_type=jnp.float32).T
-    per = width // rows
-    for k in range(per):
-        at = spot(where_ref[0], where_ref[1], pl.program_id(0) * per + k, bits)
-        block = grad[k * rows : (k + 1) * rows]
-
-        @pl.when(at < blocks // 2)
-        def _():
-            keep_ref[at] = block
-
-        @pl.when(at >= blocks // 2)
-        def _():
-            words, step = encode(block)
-            send_ref[at - blocks // 2, : rows // 2] = words
-            send_ref[at - blocks // 2, rows // 2 :] = step
-
-
-def first(hidden, latent, where, blocks):
+        [jnp.concatenate([latent[a] if a == b else zero for b in range(slots)], axis=1) for a in range(slots)], axis=0
+    )
+    for k in range(count):
+        copies[k].wait()
+        grad = jnp.dot(left, hidden[k].reshape(slots * tokens, width), preferred_element_type=jnp.float32)
+        turned[k % 2] = grad.T
+        block = turned[k % 2, pl.ds(pl.multiple_of(starts[k] - bases[k], SUB), rows)]
+        out_ref = out_refs[k // per]
+        if coded:
+            out_ref[k % per, : rows // 2], out_ref[k % per, rows // 2 :] = encode(block)
+        else:
+            out_ref[k % per] = block
+
+
+def slot_grads(hidden, latent, blocks, parts, coded):
     slots, tokens, dim = hidden.shape
     rows = dim // blocks
-    width = math.lcm(rows, LANES)
     lanes = slots * latent.shape[1]
-    return pl.pallas_call(
-        functools.partial(first_kernel, blocks, rows),
-        grid_spec=pltpu.PrefetchScalarGridSpec(
-            num_scalar_prefetch=1,
-            grid=(dim // width,),
-            in_specs=[
-                pl.BlockSpec((slots, tokens, width), lambda q, w: (0, 0, q)),
-                pl.BlockSpec(latent.shape, lambda q, w: (0, 0, 0)),
-            ],
-            out_specs=[
-                pl.BlockSpec((blocks // 2, rows, lanes), lambda q, w: (0, 0, 0)),
-                pl.BlockSpec((blocks // 2, rows // 2 + SUB, lanes), lambda q, w: (0, 0, 0)),
-            ],
-        ),
-        out_shape=[
-            jax.ShapeDtypeStruct((blocks // 2, rows, lanes), jnp.float32),
-            jax.ShapeDtypeStruct((blocks // 2, rows // 2 + SUB, lanes), jnp.int32),
+    reach = max(rows * k % LANES for k in range(blocks)) + rows
+    width = pl.cdiv(reach, LANES) * LANES
+    count = len(parts) * blocks // 4
+    shape = (
+        jax.ShapeDtypeStruct((blocks // 4, rows // 2 + SUB, lanes), jnp.int32)
+        if coded
+        else jax.ShapeDtypeStruct((blocks // 4, rows, lanes), jnp.float32)
+    )
+    return pl.pallas_call(
+        functools.partial(grad_kernel, blocks, parts, coded),
+        in_specs=[whole(pltpu.HBM), whole(pltpu.HBM)],
+        out_specs=[whole()] * len(parts),
+        out_shape=[shape] * len(parts),
+        scratch_shapes=[
+            pltpu.VMEM((count, slots, tokens, width), hidden.dtype),
+            pltpu.VMEM(latent.shape, latent.dtype),
+            pltpu.VMEM((2, width, lanes), jnp.float32),
+            pltpu.SemaphoreType.DMA((count + 1,)),
         ],
         compiler_params=params(),
-    )(where, hidden, latent)
+    )(hidden, latent)
 
 
 def added(got_ref, keep_ref, at):
@@ -138,26 +150,42 @@
     )(got, keep)
 
 
-def last_kernel(ids_ref, got_ref, keep_ref, out_ref):
+def pass_kernel(got_ref, keep_ref, send_ref):
+    half = keep_ref.shape[1] // 2
+    send_ref[0, :half], send_ref[0, half:] = encode(added(got_ref, keep_ref, 0))
+
+
+def passed(got, keep):
+    return pl.pallas_call(
+        pass_kernel,
+        in_specs=[whole(), whole()],
+        out_specs=whole(),
+        out_shape=jax.ShapeDtypeStruct(got.shape, got.dtype),
+        compiler_params=params(),
+    )(got, keep)
+
+
+def last_kernel(ids_ref, got_ref, keep_ref, across_ref, out_ref):
     rows, lanes = keep_ref.shape[1:]
-    slots = ids_ref.shape[0]
-    out_ref[:rows] = added(got_ref, keep_ref, 0)
+    slots = ids_ref.shape[1]
+    half = rows // 2
+    out_ref[:rows] = added(got_ref, keep_ref, 0) + decode(across_ref[0, :half], across_ref[0, half:])
     slot = lax.broadcasted_iota(jnp.int32, (SUB, lanes), 1) // (lanes // slots)
     row = jnp.zeros((SUB, lanes), jnp.float32)
     for s in range(slots):
-        row = jnp.where(slot == s, ids_ref[s].astype(jnp.float32), row)
+        row = jnp.where(slot == s, ids_ref[:, s : s + 1].astype(jnp.float32), row)
     out_ref[rows:] = row
 
 
-def last(ids, got, keep):
+def last(ids, got, keep, across):
     _, rows, lanes = keep.shape
     return pl.pallas_call(
         last_kernel,
-        in_specs=[whole(pltpu.SMEM), whole(), whole()],
+        in_specs=[whole(), whole(), whole(), whole()],
         out_specs=whole(),
         out_shape=jax.ShapeDtypeStruct((rows + SUB, lanes), jnp.float32),
         compiler_params=params(),
-    )(ids, got, keep)
+    )(ids, got, keep, across)
 
 
 def spread(x, rank):
@@ -279,13 +307,21 @@
         pairs = [(g * blocks + f, g * blocks + (f ^ (1 << (odd if g % 2 else even)))) for g in range(groups) for f in range(blocks)]
         return functools.partial(lax.ppermute, axis_name=BOTH, perm=pairs)
 
-    where = jnp.stack([lax.axis_index("fsdp"), lax.axis_index("language") % 2]).astype(jnp.int32)
-    keep, send = first(hidden, latent_grad.transpose(0, 2, 1), where, blocks)
-    for k in range(bits):
-        got = flip(k, 1 - k if k < 2 else k)(send)
-        if k < bits - 1:
-            keep, send = middle(got, keep)
-    mine = last(lang_ids, got, keep)
+    hidden = pltpu.with_memory_space_constraint(hidden, pltpu.HBM)
+    latent = pltpu.with_memory_space_constraint(latent_grad.transpose(0, 2, 1), pltpu.HBM)
+    stage = [flip(k, 1 - k if k < 2 else k) for k in range(bits)]
+    (send_far,) = slot_grads(hidden, latent, blocks, ((1, 1),), True)
+    far = stage[0](send_far)
+    (send_near,) = slot_grads(hidden, latent, blocks, ((0, 1),), True)
+    near = stage[0](send_near)
+    keep_far, keep_near = slot_grads(hidden, latent, blocks, ((1, 0), (0, 0)), False)
+    for k in range(1, bits - 1):
+        keep_far, send_far = middle(far, keep_far)
+        far = stage[k](send_far)
+        keep_near, send_near = middle(near, keep_near)
+        near = stage[k](send_near)
+    across = stage[bits - 1](passed(far, keep_far))
+    mine = last(lang_ids[None], near, keep_near, across)
     every = lax.all_gather(mine, "language")
     sums = dots(every, rank)
     grads = turn(every)

time: 58.6 us -> 49.8 us (0.85)
  waiting for transfers between devices: 27.3 us -> 20.2 us
  Pallas kernels: 6.89 us -> 10.4 us
  starting transfers between devices: 18.8 us -> 16.2 us
  local copies, waits for them, and re-layouts: 2.52 us -> 0.03 us
    ppermute x4 -> x7, waiting for transfers between devices: 20.2 us -> 8.76 us  [the longest x1 3.35 us: local(): across = stage[bits - 1](passed(far, keep_far))]
    ppermute x4, starting transfers between devices: 8.31 us -> 3.81 us  [local(): sums = sums + flip(k, k)(sums)]
    ppermute x4, waiting for transfers between devices: 7.1 us -> 11.4 us  [local(): sums = sums + flip(k, k)(sums)]
    pallas_call x2 -> x5, Pallas kernels: 4.74 us -> 8.34 us  [the longest x3 8.19 us: slot_grads(): pl.pallas_call(functools.partial(grad_kernel, blocks, parts, coded), in_s...]
    unnamed x14 -> x10, local copies, waits for them, and re-layouts: 2.52 us -> 0.03 us
    ppermute x4 -> x7, starting transfers between devices: 10.5 us -> 12.3 us  [the longest x2 3.73 us: local(): far = stage[k](send_far)]
  transfers between devices with their start and end apart: 8 -> 11, of which waited for: 8 -> 8; matrix products, arithmetic and copies ran while one was open for 0% -> 0% of each run, Pallas kernels for 0% -> 13%
where the time goes in v2:
time: 49.8 us; the launch traced here: 49.6 us
  waiting for transfers between devices  20.2 us (41%)
  starting transfers between devices  16.2 us (33%)
  Pallas kernels  10.4 us (21%)
  blocking collectives  2.05 us (4%)
  between operations  0.78 us (2%)
    ppermute x4, waiting for transfers between devices, local(): sums = sums + flip(k, k)(sums)  11.4 us
    pallas_call x3, Pallas kernels, slot_grads(): pl.pallas_call(functools.partial(grad_kernel, blocks, parts, coded), in_s...  8.19 us
    ppermute x4, starting transfers between devices, local(): sums = sums + flip(k, k)(sums)  3.81 us
    ppermute x2, starting transfers between devices, local(): far = stage[k](send_far)  3.73 us
    ppermute x1, waiting for transfers between devices, local(): across = stage[bits - 1](passed(far, keep_far))  3.35 us
    ppermute x1, starting transfers between devices, local(): far = stage[0](send_far)  3.03 us
    ppermute x2, starting transfers between devices, local(): near = stage[k](send_near)  2.83 us
    ppermute x1, waiting for transfers between devices, local(): near = stage[0](send_near)  2.72 us
  transfers between devices with their start and end apart: 11, of which 8 were waited for; matrix products, arithmetic and copies ran while one was open for 0% of the time, Pallas kernels for 13%

profile of v2, /device:TPU:0, one launch (start us, length us, event | category | flops | bytes accessed | tf_op | source)
XLA Modules:
  0.0 49.6 jit_solution(3518782379601489731)
XLA Ops:
  0.6 2.4 %shard_map.106 = s32[4,168,128]{2,1,0:T(8,128)S(1)} custom-call(bf16[2,128,5120]{2,1,0:T(8,128)(2,1)} %hidden_ref.5, bf16[2,64,128]{2,1,0:T(8,128)(2,1)} %bitcast.19), custom_call_target="tpu_custom_call" | custom-call | tf_op jit(solution)/shard_map/pallas_call | solution.py:108
  3.0 3.0 %collective-permute-start.3 = (s32[4,168,128]{2,1,0:T(8,128)S(1)}, s32[4,168,128]{2,1,0:T(8,128)S(1)}, u32[]{:S(2)}, u32[]{:S(2)}) collective-permute-start(s32[4,168,128]{2,1,0:T(8,128)S(1)} %shard_map.106), channel_id=1, source_target_pairs={{0,1},{1,0},{2,3},{3,2},{4,5},{5,4},{6,7},{7,6},{8,9},{9,8},{10,11... | collective-permute-start | bytes 1032200 | tf_op jit(solution)/shard_map/ppermute | solution.py:314
  6.1 2.4 %shard_map.102 = s32[4,168,128]{2,1,0:T(8,128)S(1)} custom-call(bf16[2,128,5120]{2,1,0:T(8,128)(2,1)} %hidden_ref.5, bf16[2,64,128]{2,1,0:T(8,128)(2,1)} %bitcast.20), custom_call_target="tpu_custom_call" | custom-call | tf_op jit(solution)/shard_map/pallas_call | solution.py:108
  8.6 3.4 %shard_map.103 = (f32[4,320,128]{2,1,0:T(8,128)S(1)}, f32[4,320,128]{2,1,0:T(8,128)S(1)}) custom-call(bf16[2,128,5120]{2,1,0:T(8,128)(2,1)} %hidden_ref.5, bf16[2,64,128]{2,1,0:T(8,128)(2,1)} %bitcast.21), custom_call_target="tpu_custom_call" | custom-call | tf_op jit(solution)/shard_map/pallas_call | solution.py:108
  12.0 0.2 shard_map.107
  12.2 2.1 %collective-permute-start.4 = (s32[2,168,128]{2,1,0:T(8,128)S(1)}, s32[2,168,128]{2,1,0:T(8,128)S(1)}, u32[]{:S(2)}, u32[]{:S(2)}) collective-permute-start(s32[2,168,128]{2,1,0:T(8,128)S(1)} %get-tuple-element.24), channel_id=1, source_target_pairs={{0,2},{1,3},{2,0},{3,1},{4,6},{5,7},{6,4},{7,5},{8,10},{9,11},{10,... | collective-permute-start | bytes 516104 | tf_op jit(solution)/shard_map/ppermute | solution.py:320
  14.3 2.7 %collective-permute-done.got_ref = s32[4,168,128]{2,1,0:T(8,128)S(1)} collective-permute-done((s32[4,168,128]{2,1,0:T(8,128)S(1)}, s32[4,168,128]{2,1,0:T(8,128)S(1)}, u32[]{:S(2)}, u32[]{:S(2)}) %collective-permute-start) | collective-permute-done | bytes 344096 | tf_op jit(solution)/shard_map/ppermute | solution.py:316
  17.1 0.2 shard_map.104
  17.3 1.4 %collective-permute-start.1 = (s32[2,168,128]{2,1,0:T(8,128)S(1)}, s32[2,168,128]{2,1,0:T(8,128)S(1)}, u32[]{:S(2)}, u32[]{:S(2)}) collective-permute-start(s32[2,168,128]{2,1,0:T(8,128)S(1)} %get-tuple-element.19), channel_id=1, source_target_pairs={{0,2},{1,3},{2,0},{3,1},{4,6},{5,7},{6,4},{7,5},{8,10},{9,11},{10,... | collective-permute-start | bytes 516104 | tf_op jit(solution)/shard_map/ppermute | solution.py:322
  18.8 1.6 %collective-permute-start.5 = (s32[1,168,128]{2,1,0:T(8,128)S(1)}, s32[1,168,128]{2,1,0:T(8,128)S(1)}, u32[]{:S(2)}, u32[]{:S(2)}) collective-permute-start(s32[1,168,128]{2,1,0:T(8,128)S(1)} %get-tuple-element.26), channel_id=1, source_target_pairs={{0,4},{1,5},{2,6},{3,7},{4,0},{5,1},{6,2},{7,3},{8,12},{9,13},{10,... | collective-permute-start | bytes 258056 | tf_op jit(solution)/shard_map/ppermute | solution.py:320
  20.4 2.3 %collective-permute-done.1.got_ref = s32[2,168,128]{2,1,0:T(8,128)S(1)} collective-permute-done((s32[2,168,128]{2,1,0:T(8,128)S(1)}, s32[2,168,128]{2,1,0:T(8,128)S(1)}, u32[]{:S(2)}, u32[]{:S(2)}) %collective-permute-start.1) | collective-permute-done | bytes 172064 | tf_op jit(solution)/shard_map/ppermute | solution.py:322
  22.9 1.4 %collective-permute-start.2 = (s32[1,168,128]{2,1,0:T(8,128)S(1)}, s32[1,168,128]{2,1,0:T(8,128)S(1)}, u32[]{:S(2)}, u32[]{:S(2)}) collective-permute-start(s32[1,168,128]{2,1,0:T(8,128)S(1)} %get-tuple-element.21), channel_id=1, source_target_pairs={{0,4},{1,5},{2,6},{3,7},{4,0},{5,1},{6,2},{7,3},{8,12},{9,13},{10,... | collective-permute-start | bytes 258056 | tf_op jit(solution)/shard_map/ppermute | solution.py:322
  24.4 2.7 %collective-permute-start.6 = (s32[1,168,128]{2,1,0:T(8,128)S(1)}, s32[1,168,128]{2,1,0:T(8,128)S(1)}, u32[]{:S(2)}, u32[]{:S(2)}) collective-permute-start(s32[1,168,128]{2,1,0:T(8,128)S(1)} %shard_map.109), channel_id=1, source_target_pairs={{0,8},{1,9},{2,10},{3,11},{4,12},{5,13},{6,14},{7,15},{8,0},{9,1},... | collective-permute-start | bytes 258056 | tf_op jit(solution)/shard_map/ppermute | solution.py:323
  27.0 0.4 collective-permute-done.2.got_ref
  27.4 3.4 %collective-permute-done.6.across_ref = s32[1,168,128]{2,1,0:T(8,128)S(1)} collective-permute-done((s32[1,168,128]{2,1,0:T(8,128)S(1)}, s32[1,168,128]{2,1,0:T(8,128)S(1)}, u32[]{:S(2)}, u32[]{:S(2)}) %collective-permute-start.6) | collective-permute-done | bytes 86048 | tf_op jit(solution)/shard_map/ppermute | solution.py:323
  30.8 2.0 %all-gather = f32[656,128]{1,0:T(8,128)S(1)} all-gather(f32[328,128]{1,0:T(8,128)S(1)} %shard_map.110), channel_id=2, replica_groups=mesh['language'=2,'fsdp'=16] {'language'}, dimensions={0}, use_global_device_ids=true | all-gather | bytes 503808 | tf_op jit(solution)/shard_map/all_gather | solution.py:325
  33.1 3.6 %collective-permute-done.7 = f32[8,128]{1,0:T(8,128)S(1)} collective-permute-done((f32[8,128]{1,0:T(8,128)S(1)}, f32[8,128]{1,0:T(8,128)S(1)}, u32[]{:S(2)}, u32[]{:S(2)}) %collective-permute-start.7) | collective-permute-done | bytes 4128 | tf_op jit(solution)/shard_map/ppermute | solution.py:329
  36.7 1.5 %collective-permute-start.8 = (f32[8,128]{1,0:T(8,128)S(1)}, f32[8,128]{1,0:T(8,128)S(1)}, u32[]{:S(2)}, u32[]{:S(2)}) collective-permute-start(f32[8,128]{1,0:T(8,128)S(1)} %add.12), channel_id=1, source_target_pairs={{0,2},{1,3},{2,0},{3,1},{4,6},{5,7},{6,4},{7,5},{8,10},{9,11},{10,... | collective-permute-start | bytes 12296 | tf_op jit(solution)/shard_map/ppermute | solution.py:329
  38.2 2.1 %collective-permute-done.8 = f32[8,128]{1,0:T(8,128)S(1)} collective-permute-done((f32[8,128]{1,0:T(8,128)S(1)}, f32[8,128]{1,0:T(8,128)S(1)}, u32[]{:S(2)}, u32[]{:S(2)}) %collective-permute-start.8) | collective-permute-done | bytes 4128 | tf_op jit(solution)/shard_map/ppermute | solution.py:329
  40.3 0.4 collective-permute-start.9
  40.7 3.2 %collective-permute-done.9 = f32[8,128]{1,0:T(8,128)S(1)} collective-permute-done((f32[8,128]{1,0:T(8,128)S(1)}, f32[8,128]{1,0:T(8,128)S(1)}, u32[]{:S(2)}, u32[]{:S(2)}) %collective-permute-start.9) | collective-permute-done | bytes 4128 | tf_op jit(solution)/shard_map/ppermute | solution.py:329
  43.9 1.8 %collective-permute-start.10 = (f32[8,128]{1,0:T(8,128)S(1)}, f32[8,128]{1,0:T(8,128)S(1)}, u32[]{:S(2)}, u32[]{:S(2)}) collective-permute-start(f32[8,128]{1,0:T(8,128)S(1)} %add.14), channel_id=1, source_target_pairs={{0,8},{1,9},{2,10},{3,11},{4,12},{5,13},{6,14},{7,15},{8,0},{9,1},... | collective-permute-start | bytes 12296 | tf_op jit(solution)/shard_map/ppermute | solution.py:329
  45.9 2.6 %collective-permute-done.10 = f32[8,128]{1,0:T(8,128)S(1)} collective-permute-done((f32[8,128]{1,0:T(8,128)S(1)}, f32[8,128]{1,0:T(8,128)S(1)}, u32[]{:S(2)}, u32[]{:S(2)}) %collective-permute-start.10) | collective-permute-done | bytes 4128 | tf_op jit(solution)/shard_map/ppermute | solution.py:329
  48.5 1.1 %shard_map.113 = (f32[64,320]{1,0:T(8,128)}, f32[64,320]{1,0:T(8,128)}, f32[64,320]{1,0:T(8,128)}, f32[1,4]{1,0:T(1,128)}) custom-call(f32[8,128]{1,0:T(8,128)S(1)} %add.15.sums_ref, f32[2,328,128]{2,1,0:T(8,128)S(1)} %bitcast.13, f32[2,128,320]{2,1,0:T(8,128)S(1)} %shard_map.112.grad_ref, f32[1,4]{1,0:T(1,128)S(1)} %bitcast.17, f32[64,320]{1,0:T(8,128)S(1)} %bitcast.14, ...), custom_call_target="tpu_custom_call" | custom-call | tf_op jit(solution)/shard_map/pallas_call | solution.py:284
  (25 shorter events, 0.9 us)
Async XLA Ops:
  3.0 9.0 %collective-permute-start.3 = (s32[4,168,128]{2,1,0:T(8,128)S(1)}, s32[4,168,128]{2,1,0:T(8,128)S(1)}, u32[]{:S(2)}, u32[]{:S(2)}) collective-permute-start(s32[4,168,128]{2,1,0:T(8,128)S(1)} %shard_map.106), channel_id=1, source_target_pairs={{0,1},{1,0},{2,3},{3,2},{4,5},{5,4},{6,7},{7,6},{8,9},{9,8},{10,11... | collective-permute-start | bytes 1032200 | tf_op jit(solution)/shard_map/ppermute | solution.py:314
  8.4 22.3 %copy-start.4 = (s32[2]{0:T(128)S(1)}, s32[2]{0:T(128)}, u32[]{:S(2)}) copy-start(s32[2]{0:T(128)} %param.9) | copy-start | bytes 28
  8.5 8.6 %collective-permute-start = (s32[4,168,128]{2,1,0:T(8,128)S(1)}, s32[4,168,128]{2,1,0:T(8,128)S(1)}, u32[]{:S(2)}, u32[]{:S(2)}) collective-permute-start(s32[4,168,128]{2,1,0:T(8,128)S(1)} %shard_map.102), channel_id=1, source_target_pairs={{0,1},{1,0},{2,3},{3,2},{4,5},{5,4},{6,7},{7,6},{8,9},{9,8},{10,11... | collective-permute-start | bytes 1032200 | tf_op jit(solution)/shard_map/ppermute | solution.py:316
  12.0 36.4 %copy-start = (f32[320,64]{0,1:T(8,128)S(1)}, f32[320,64]{0,1:T(8,128)}, u32[]{:S(2)}) copy-start(f32[320,64]{0,1:T(8,128)} %param.11) | copy-start | bytes 245764
  12.0 36.4 %copy-start.1 = (f32[320,64]{0,1:T(8,128)S(1)}, f32[320,64]{0,1:T(8,128)}, u32[]{:S(2)}) copy-start(f32[320,64]{0,1:T(8,128)} %param.12) | copy-start | bytes 245764
  12.0 36.4 %copy-start.2 = (f32[320,64]{0,1:T(8,128)S(1)}, f32[320,64]{0,1:T(8,128)}, u32[]{:S(2)}) copy-start(f32[320,64]{0,1:T(8,128)} %param.13) | copy-start | bytes 245764
  12.0 36.4 %copy-start.3 = (f32[4]{0:T(128)S(1)}, f32[4]{0:T(128)}, u32[]{:S(2)}) copy-start(f32[4]{0:T(128)} %param.10) | copy-start | bytes 52
  12.2 6.4 %collective-permute-start.4 = (s32[2,168,128]{2,1,0:T(8,128)S(1)}, s32[2,168,128]{2,1,0:T(8,128)S(1)}, u32[]{:S(2)}, u32[]{:S(2)}) collective-permute-start(s32[2,168,128]{2,1,0:T(8,128)S(1)} %get-tuple-element.24), channel_id=1, source_target_pairs={{0,2},{1,3},{2,0},{3,1},{4,6},{5,7},{6,4},{7,5},{8,10},{9,11},{10,... | collective-permute-start | bytes 516104 | tf_op jit(solution)/shard_map/ppermute | solution.py:320
  17.3 5.5 %collective-permute-start.1 = (s32[2,168,128]{2,1,0:T(8,128)S(1)}, s32[2,168,128]{2,1,0:T(8,128)S(1)}, u32[]{:S(2)}, u32[]{:S(2)}) collective-permute-start(s32[2,168,128]{2,1,0:T(8,128)S(1)} %get-tuple-element.19), channel_id=1, source_target_pairs={{0,2},{1,3},{2,0},{3,1},{4,6},{5,7},{6,4},{7,5},{8,10},{9,11},{10,... | collective-permute-start | bytes 516104 | tf_op jit(solution)/shard_map/ppermute | solution.py:322
  18.8 5.5 %collective-permute-start.5 = (s32[1,168,128]{2,1,0:T(8,128)S(1)}, s32[1,168,128]{2,1,0:T(8,128)S(1)}, u32[]{:S(2)}, u32[]{:S(2)}) collective-permute-start(s32[1,168,128]{2,1,0:T(8,128)S(1)} %get-tuple-element.26), channel_id=1, source_target_pairs={{0,4},{1,5},{2,6},{3,7},{4,0},{5,1},{6,2},{7,3},{8,12},{9,13},{10,... | collective-permute-start | bytes 258056 | tf_op jit(solution)/shard_map/ppermute | solution.py:320
  22.9 4.6 %collective-permute-start.2 = (s32[1,168,128]{2,1,0:T(8,128)S(1)}, s32[1,168,128]{2,1,0:T(8,128)S(1)}, u32[]{:S(2)}, u32[]{:S(2)}) collective-permute-start(s32[1,168,128]{2,1,0:T(8,128)S(1)} %get-tuple-element.21), channel_id=1, source_target_pairs={{0,4},{1,5},{2,6},{3,7},{4,0},{5,1},{6,2},{7,3},{8,12},{9,13},{10,... | collective-permute-start | bytes 258056 | tf_op jit(solution)/shard_map/ppermute | solution.py:322
  24.4 6.4 %collective-permute-start.6 = (s32[1,168,128]{2,1,0:T(8,128)S(1)}, s32[1,168,128]{2,1,0:T(8,128)S(1)}, u32[]{:S(2)}, u32[]{:S(2)}) collective-permute-start(s32[1,168,128]{2,1,0:T(8,128)S(1)} %shard_map.109), channel_id=1, source_target_pairs={{0,8},{1,9},{2,10},{3,11},{4,12},{5,13},{6,14},{7,15},{8,0},{9,1},... | collective-permute-start | bytes 258056 | tf_op jit(solution)/shard_map/ppermute | solution.py:323
  33.0 3.7 %collective-permute-start.7 = (f32[8,128]{1,0:T(8,128)S(1)}, f32[8,128]{1,0:T(8,128)S(1)}, u32[]{:S(2)}, u32[]{:S(2)}) collective-permute-start(f32[8,128]{1,0:T(8,128)S(1)} %shard_map.111), channel_id=1, source_target_pairs={{0,1},{1,0},{2,3},{3,2},{4,5},{5,4},{6,7},{7,6},{8,9},{9,8},{10,11... | collective-permute-start | bytes 12296 | tf_op jit(solution)/shard_map/ppermute | solution.py:329
  36.7 3.6 %collective-permute-start.8 = (f32[8,128]{1,0:T(8,128)S(1)}, f32[8,128]{1,0:T(8,128)S(1)}, u32[]{:S(2)}, u32[]{:S(2)}) collective-permute-start(f32[8,128]{1,0:T(8,128)S(1)} %add.12), channel_id=1, source_target_pairs={{0,2},{1,3},{2,0},{3,1},{4,6},{5,7},{6,4},{7,5},{8,10},{9,11},{10,... | collective-permute-start | bytes 12296 | tf_op jit(solution)/shard_map/ppermute | solution.py:329
  40.3 3.6 %collective-permute-start.9 = (f32[8,128]{1,0:T(8,128)S(1)}, f32[8,128]{1,0:T(8,128)S(1)}, u32[]{:S(2)}, u32[]{:S(2)}) collective-permute-start(f32[8,128]{1,0:T(8,128)S(1)} %add.13), channel_id=1, source_target_pairs={{0,4},{1,5},{2,6},{3,7},{4,0},{5,1},{6,2},{7,3},{8,12},{9,13},{10,... | collective-permute-start | bytes 12296 | tf_op jit(solution)/shard_map/ppermute | solution.py:329
  43.9 4.5 %collective-permute-start.10 = (f32[8,128]{1,0:T(8,128)S(1)}, f32[8,128]{1,0:T(8,128)S(1)}, u32[]{:S(2)}, u32[]{:S(2)}) collective-permute-start(f32[8,128]{1,0:T(8,128)S(1)} %add.14), channel_id=1, source_target_pairs={{0,8},{1,9},{2,10},{3,11},{4,12},{5,13},{6,14},{7,15},{8,0},{9,1},... | collective-permute-start | bytes 12296 | tf_op jit(solution)/shard_map/ppermute | solution.py:329

commit v3 on v2

v3 whole, which is shorter than its diff:
```python
import functools

import jax
import jax.numpy as jnp
from jax import lax
from jax.experimental import pallas as pl
from jax.experimental.pallas import tpu as pltpu
from jax.sharding import PartitionSpec as P


STEP = 100
SUB = 8
LANES = 128
FINE = 32.0
TOP = 32766.0
VMEM_LIMIT = 24 * 1024 * 1024
BOTH = ("language", "fsdp")


def whole(memory=pltpu.VMEM):
    return pl.BlockSpec(memory_space=memory)


def params():
    return pltpu.CompilerParams(vmem_limit_bytes=VMEM_LIMIT)


def encode(block):
    rows, lanes = block.shape
    half = rows // 2
    top = jnp.max(jnp.abs(block).reshape(rows // SUB, SUB, lanes), axis=0)
    step = jnp.ceil(jnp.log2(jnp.maximum(top, 1e-30)) * FINE)
    scale = jnp.exp2(step * (-1.0 / FINE)) * TOP
    codes = block.reshape(rows // SUB, SUB, lanes) * scale[None] + 32768.5
    codes = codes.astype(jnp.int32).reshape(rows, lanes)
    words = lax.shift_left(codes[:half], 16) | codes[half:]
    return words, step.astype(jnp.int32)


def decode(words, step):
    half, lanes = words.shape
    scale = jnp.exp2(step.astype(jnp.float32) * (1.0 / FINE)) * (1.0 / TOP)
    high = lax.shift_right_logical(words, 16).astype(jnp.float32) - 32768.0
    low = (words & 65535).astype(jnp.float32) - 32768.0
    both = jnp.concatenate([high, low], axis=0).reshape(2 * half // SUB, SUB, lanes)
    return (both * scale[None]).reshape(2 * half, lanes)


def place(blocks, parity, chain, half, index):
    bits = blocks.bit_length() - 1
    p = (half << parity) | (chain << (bits - 1))
    for k in range(1, bits - 1):
        bit = (index >> (bits - 2 - k)) & 1
        p |= bit << (1 - parity if k == 1 else k)
    return p


def grad_kernel(blocks, parts, coded, hidden_ref, latent_ref, *refs):
    out_refs, (hidden, latent, turned, sems) = refs[: len(parts)], refs[len(parts) :]
    count, slots, tokens, width = hidden.shape
    rank = latent.shape[1]
    rows = hidden_ref.shape[2] // blocks
    per = blocks // 4
    me, odd = lax.axis_index("fsdp"), lax.axis_index("language") % 2 == 1
    starts = []
    for chain, half in parts:
        for k in range(per):
            at_even, at_odd = place(blocks, 0, chain, half, k), place(blocks, 1, chain, half, k)
            starts.append(jnp.bitwise_xor(me, jnp.where(odd, at_odd, at_even)) * rows)
    small = pltpu.make_async_copy(latent_ref, latent, sems.at[count])
    small.start()
    copies, bases = [], []
    for k in range(count):
        base = jnp.minimum(starts[k] // LANES, (hidden_ref.shape[2] - width) // LANES) * LANES
        bases.append(pl.multiple_of(base, LANES))
        base = bases[k]
        copies.append(pltpu.make_async_copy(hidden_ref.at[:, :, pl.ds(base, width)], hidden.at[k], sems.at[k]))
        copies[k].start()
    small.wait()
    zero = jnp.zeros((rank, tokens), latent.dtype)
    left = jnp.concatenate(
        [jnp.concatenate([latent[a] if a == b else zero for b in range(slots)], axis=1) for a in range(slots)], axis=0
    )
    for k in range(count):
        copies[k].wait()
    for k in range(count):
        grad = jnp.dot(left, hidden[k].reshape(slots * tokens, width), preferred_element_type=jnp.float32)
        turned[k] = grad.T
    for k in range(count):
        block = turned[k, pl.ds(pl.multiple_of(starts[k] - bases[k], SUB), rows)]
        out_ref = out_refs[k // per]
        if coded:
            out_ref[k % per, : rows // 2], out_ref[k % per, rows // 2 :] = encode(block)
        else:
            out_ref[k % per] = block


def slot_grads(hidden, latent, blocks, parts, coded):
    slots, tokens, dim = hidden.shape
    rows = dim // blocks
    lanes = slots * latent.shape[1]
    reach = max(rows * k % LANES for k in range(blocks)) + rows
    width = pl.cdiv(reach, LANES) * LANES
    count = len(parts) * blocks // 4
    shape = (
        jax.ShapeDtypeStruct((blocks // 4, rows // 2 + SUB, lanes), jnp.int32)
        if coded
        else jax.ShapeDtypeStruct((blocks // 4, rows, lanes), jnp.float32)
    )
    return pl.pallas_call(
        functools.partial(grad_kernel, blocks, parts, coded),
        in_specs=[whole(pltpu.HBM), whole(pltpu.HBM)],
        out_specs=[whole()] * len(parts),
        out_shape=[shape] * len(parts),
        scratch_shapes=[
            pltpu.VMEM((count, slots, tokens, width), hidden.dtype),
            pltpu.VMEM(latent.shape, latent.dtype),
            pltpu.VMEM((count, width, lanes), jnp.float32),
            pltpu.SemaphoreType.DMA((count + 1,)),
        ],
        compiler_params=params(),
    )(hidden, latent)


def added(got_ref, keep_ref, at):
    half = got_ref.shape[1] - SUB
    return keep_ref[at] + decode(got_ref[at, :half], got_ref[at, half:])


def middle_kernel(got_ref, keep_ref, *refs):
    left_ref, send_ref = refs[-2:]
    blocks = keep_ref.shape[0]
    half = keep_ref.shape[1] // 2
    for k in range(blocks // 2):
        words, step = encode(added(got_ref, keep_ref, blocks // 2 + k))
        send_ref[k, :half] = words
        send_ref[k, half:] = step
    for k in range(blocks // 2):
        left_ref[k] = added(got_ref, keep_ref, k)


def middle(got, keep, *after):
    blocks, rows, lanes = keep.shape
    return pl.pallas_call(
        middle_kernel,
        in_specs=[whole(), whole()] + [whole(pl.ANY)] * len(after),
        out_specs=[whole(), whole()],
        out_shape=[
            jax.ShapeDtypeStruct((blocks // 2, rows, lanes), jnp.float32),
            jax.ShapeDtypeStruct((blocks // 2, rows // 2 + SUB, lanes), jnp.int32),
        ],
        compiler_params=params(),
    )(got, keep, *after)


def pass_kernel(got_ref, keep_ref, send_ref):
    half = keep_ref.shape[1] // 2
    send_ref[0, :half], send_ref[0, half:] = encode(added(got_ref, keep_ref, 0))


def passed(got, keep):
    return pl.pallas_call(
        pass_kernel,
        in_specs=[whole(), whole()],
        out_specs=whole(),
        out_shape=jax.ShapeDtypeStruct(got.shape, got.dtype),
        compiler_params=params(),
    )(got, keep)


def last_kernel(got_ref, keep_ref, across_ref, out_ref):
    half = keep_ref.shape[1] // 2
    out_ref[...] = added(got_ref, keep_ref, 0) + decode(across_ref[0, :half], across_ref[0, half:])


def last(got, keep, across):
    return pl.pallas_call(
        last_kernel,
        in_specs=[whole(), whole(), whole()],
        out_specs=whole(),
        out_shape=jax.ShapeDtypeStruct(keep.shape[1:], jnp.float32),
        compiler_params=params(),
    )(got, keep, across)


def spread(x, rank):
    lanes = x.shape[1]
    out = x
    shift = rank
    while shift < lanes:
        out = out + pltpu.roll(out, shift, 1)
        shift *= 2
    return out


def parity():
    return lax.axis_index("language") % 2


def positions(count):
    return (parity(), 1 - parity()) if count == 2 else tuple(range(count))


def dots_kernel(rank, *refs):
    grad_refs, out_ref = refs[:-1], refs[-1]
    groups = len(grad_refs)
    total = grad_refs[0][...]
    for ref in grad_refs[1:]:
        total = total + ref[...]
    total = spread(total, rank)
    row = lax.broadcasted_iota(jnp.int32, out_ref.shape, 0)
    out = jnp.where(row == groups, jnp.sum(total * total, axis=0, keepdims=True), 0.0)
    for at, ref in zip(positions(groups), grad_refs):
        out = jnp.where(row == at, jnp.sum(ref[...] * total, axis=0, keepdims=True), out)
    out_ref[...] = out


def dots(every, rank):
    return pl.pallas_call(
        functools.partial(dots_kernel, rank),
        in_specs=[whole()] * len(every),
        out_specs=whole(),
        out_shape=jax.ShapeDtypeStruct((pl.cdiv(len(every) + 1, SUB) * SUB, every[0].shape[1]), jnp.float32),
        compiler_params=params(),
    )(*every)


def turn_kernel(*refs):
    for at, ref in zip(positions(len(refs) - 1), refs):
        refs[-1][at] = ref[...].T


def turn(every):
    rows, lanes = every[0].shape
    return pl.pallas_call(
        turn_kernel,
        in_specs=[whole()] * len(every),
        out_specs=whole(),
        out_shape=jax.ShapeDtypeStruct((len(every), lanes, rows), jnp.float32),
        compiler_params=params(),
    )(*every)


def final_kernel(
    groups,
    sums_ref,
    got_ref,
    grad_ref,
    old_ref,
    param_ref,
    first_ref,
    second_ref,
    *refs,
):
    ids_refs, (new_param_ref, new_first_ref, new_second_ref, log_ref) = refs[:groups], refs[groups:]
    lanes = grad_ref.shape[1]
    langs = old_ref.shape[1]
    rank = param_ref.shape[0]
    slots = lanes // rank
    sums = sums_ref[...] + got_ref[...]
    parts = sums[:groups]
    square = jnp.sum(sums[groups : groups + 1, :rank], axis=1, keepdims=True) + 1e-06
    slot = lax.broadcasted_iota(jnp.int32, (groups, lanes), 1) // rank
    row = lax.broadcasted_iota(jnp.int32, (groups, lanes), 0)
    ids = jnp.zeros((groups, lanes), jnp.int32)
    for at, ref in zip(positions(groups), ids_refs):
        for k in range(slots):
            ids = jnp.where((slot == k) & (row == at), ref[:, k : k + 1], ids)
    at = lax.broadcasted_iota(jnp.int32, (1, langs), 1)
    align = jnp.zeros((1, langs), jnp.float32)
    for k in range(langs):
        one = jnp.sum(jnp.where(ids == k, parts, 0.0), axis=0, keepdims=True)
        align = jnp.where(at == k, jnp.sum(one, axis=1, keepdims=True), align)
    logits = jnp.log(old_ref[...]) + float(langs) * (align / square)
    logs = logits - jnp.log(jnp.sum(jnp.exp(logits), axis=1, keepdims=True))
    log_ref[...] = logs
    weights = jnp.exp(logs)
    update = None
    for g in range(groups):
        for s in range(slots):
            own = ids[g : g + 1, s * rank : s * rank + 1]
            weight = jnp.zeros((1, 1), jnp.float32)
            for k in range(langs):
                weight = weight + jnp.where(own == k, weights[:, k : k + 1], 0.0)
            term = weight * grad_ref[g, s * rank : (s + 1) * rank]
            update = term if update is None else update + term
    new_first = 0.9 * first_ref[...] + 0.1 * update
    new_second = 0.95 * second_ref[...] + 0.05 * update * update
    first_hat = new_first / (1.0 - 0.9**STEP)
    second_hat = new_second / (1.0 - 0.95**STEP)
    param = param_ref[...]
    new_param_ref[...] = param - 0.02 * (first_hat / (jnp.sqrt(second_hat) + 1e-08) + 0.1 * param)
    new_first_ref[...] = new_first
    new_second_ref[...] = new_second


def final(sums, got, grads, ids, old, param, first_moment, second_moment):
    shape = jax.ShapeDtypeStruct(param.shape, jnp.float32)
    return pl.pallas_call(
        functools.partial(final_kernel, len(ids)),
        in_specs=[whole()] * (7 + len(ids)),
        out_specs=[whole()] * 4,
        out_shape=[shape, shape, shape, jax.ShapeDtypeStruct(old.shape, jnp.float32)],
        compiler_params=params(),
    )(sums, got, grads, old, param, first_moment, second_moment, *ids)


def local(groups, blocks, hidden, latent_grad, lang_ids, old_weights, param, first_moment, second_moment):
    bits = blocks.bit_length() - 1
    rank = latent_grad.shape[2]

    def swap(x, even, odd, cross=0):
        pairs = []
        for g in range(groups):
            bit = odd if g % 2 else even
            pairs += [(g * blocks + f, (g ^ cross) * blocks + (f if bit is None else f ^ (1 << bit))) for f in range(blocks)]
        return lax.ppermute(x, BOTH, pairs)

    hidden = pltpu.with_memory_space_constraint(hidden, pltpu.HBM)
    latent = pltpu.with_memory_space_constraint(latent_grad.transpose(0, 2, 1), pltpu.HBM)
    far, near = 1, 0
    got, keep = {}, {}
    for c in (far, near):
        (out,) = slot_grads(hidden, latent, blocks, ((c, 1),), True)
        got[c] = swap(out, 0, 1)
    for c in (far, near):
        (keep[c],) = slot_grads(hidden, latent, blocks, ((c, 0),), False)
    ahead = []
    for k in range(1, bits):
        if k < bits - 1:
            keep[far], out = middle(got[far], keep[far])
        else:
            out = passed(got[far], keep[far])
        got[far] = swap(out, 1 if k == 1 else k, 0 if k == 1 else k)
        ahead.append(out)
    for k in range(1, bits - 1):
        keep[near], out = middle(got[near], keep[near], ahead[k])
        got[near] = swap(out, 1 if k == 1 else k, 0 if k == 1 else k)
    across = got[far]
    mine = last(got[near], keep[near], across)
    ids = lang_ids[None]
    if groups == 2:
        every = (mine, swap(mine, None, None, 1))
        ids = (ids, swap(ids, None, None, 1))
    else:
        every = tuple(lax.all_gather(mine, "language"))
        ids = tuple(lax.all_gather(ids, "language"))
    sums = dots(every, rank)
    grads = turn(every)
    for k in reversed(range(bits)):
        got = swap(sums, k, k, 1)
        if k > 0:
            sums = sums + got
    new_param, new_first, new_second, logs = final(
        sums, got, grads, ids, old_weights[None], param.T, first_moment.T, second_moment.T
    )
    return new_param.T, new_first.T, new_second.T, logs[0]


def solution(mesh):
    placed = (
        P("language", "fsdp", None),
        P("language", "fsdp", None),
        P("language"),
        P(),
        P("fsdp", None),
        P("fsdp", None),
        P("fsdp", None),
    )
    groups, blocks = mesh.shape["language"], mesh.shape["fsdp"]
    return jax.shard_map(
        functools.partial(local, groups, blocks),
        mesh=mesh,
        in_specs=placed,
        out_specs=(P("fsdp", None), P("fsdp", None), P("fsdp", None), P()),
        check_vma=False,
    )
```

time: 49.8 us -> 47.1 us (0.946)
  starting transfers between devices: 16.2 us -> 18.3 us
  blocking collectives: 2.05 us -> 0 us
  waiting for transfers between devices: 20.2 us -> 18.2 us
  Pallas kernels: 10.4 us -> 9.58 us
    ppermute x11 -> x13, starting transfers between devices: 16.2 us -> 18.3 us  [swap(): return lax.ppermute(x, BOTH, pairs)]
    all_gather x1 -> x0, blocking collectives: 2.05 us -> none  [local(): every = lax.all_gather(mine, 'language')]
    ppermute x11 -> x13, waiting for transfers between devices: 20.2 us -> 18.2 us  [swap(): return lax.ppermute(x, BOTH, pairs)]
    pallas_call x3 -> x4, Pallas kernels: 8.19 us -> 7.31 us  [slot_grads(): pl.pallas_call(functools.partial(grad_kernel, blocks, parts, coded), in_s...]
  transfers between devices with their start and end apart: 11 -> 13, of which waited for: 8 -> 11; matrix products, arithmetic and copies ran while one was open for 0% -> 0% of each run, Pallas kernels for 13% -> 13%
where the time goes in v3:
time: 47.1 us; the launch traced here: 46.9 us
  starting transfers between devices  18.3 us (39%)
  waiting for transfers between devices  18.2 us (39%)
  Pallas kernels  9.58 us (20%)
  between operations  0.79 us (2%)
    ppermute x13, starting transfers between devices, swap(): return lax.ppermute(x, BOTH, pairs)  18.3 us
    ppermute x13, waiting for transfers between devices, swap(): return lax.ppermute(x, BOTH, pairs)  18.2 us
    pallas_call x4, Pallas kernels, slot_grads(): pl.pallas_call(functools.partial(grad_kernel, blocks, parts, coded), in_s...  7.31 us
    pallas_call x1, Pallas kernels, final(): pl.pallas_call(functools.partial(final_kernel, len(ids)), in_specs=[whole...  1.21 us
  transfers between devices with their start and end apart: 13, of which 11 were waited for; matrix products, arithmetic and copies ran while one was open for 0% of the time, Pallas kernels for 13%

profile of v3, /device:TPU:0, one launch (start us, length us, event | category | flops | bytes accessed | tf_op | source)
XLA Modules:
  0.0 46.9 jit_solution(8571176632227112451)
XLA Ops:
  0.6 1.9 %shard_map.104 = s32[4,168,128]{2,1,0:T(8,128)S(1)} custom-call(bf16[2,128,5120]{2,1,0:T(8,128)(2,1)} %hidden_ref.7, bf16[2,64,128]{2,1,0:T(8,128)(2,1)} %bitcast.16), custom_call_target="tpu_custom_call" | custom-call | tf_op jit(solution)/shard_map/pallas_call | solution.py:110
  2.5 3.0 %collective-permute-start.1 = (s32[4,168,128]{2,1,0:T(8,128)S(1)}, s32[4,168,128]{2,1,0:T(8,128)S(1)}, u32[]{:S(2)}, u32[]{:S(2)}) collective-permute-start(s32[4,168,128]{2,1,0:T(8,128)S(1)} %shard_map.104), channel_id=1, source_target_pairs={{0,1},{1,0},{2,3},{3,2},{4,5},{5,4},{6,7},{7,6},{8,9},{9,8},{10,11... | collective-permute-start | bytes 1032200 | tf_op jit(solution)/shard_map/ppermute | solution.py:317
  5.6 1.9 %shard_map.102 = s32[4,168,128]{2,1,0:T(8,128)S(1)} custom-call(bf16[2,128,5120]{2,1,0:T(8,128)(2,1)} %hidden_ref.7, bf16[2,64,128]{2,1,0:T(8,128)(2,1)} %bitcast.17), custom_call_target="tpu_custom_call" | custom-call | tf_op jit(solution)/shard_map/pallas_call | solution.py:110
  7.6 1.8 %shard_map.105.keep_ref = f32[4,320,128]{2,1,0:T(8,128)S(1)} custom-call(bf16[2,128,5120]{2,1,0:T(8,128)(2,1)} %hidden_ref.7, bf16[2,64,128]{2,1,0:T(8,128)(2,1)} %bitcast.18), custom_call_target="tpu_custom_call" | custom-call | tf_op jit(solution)/shard_map/pallas_call | solution.py:110
  9.3 1.5 %collective-permute-done.1.got_ref = s32[4,168,128]{2,1,0:T(8,128)S(1)} collective-permute-done((s32[4,168,128]{2,1,0:T(8,128)S(1)}, s32[4,168,128]{2,1,0:T(8,128)S(1)}, u32[]{:S(2)}, u32[]{:S(2)}) %collective-permute-start.1) | collective-permute-done | bytes 344096 | tf_op jit(solution)/shard_map/ppermute | solution.py:317
  11.0 2.1 %collective-permute-start.2 = (s32[2,168,128]{2,1,0:T(8,128)S(1)}, s32[2,168,128]{2,1,0:T(8,128)S(1)}, u32[]{:S(2)}, u32[]{:S(2)}) collective-permute-start(s32[2,168,128]{2,1,0:T(8,128)S(1)} %get-tuple-element.16), channel_id=1, source_target_pairs={{0,2},{1,3},{2,0},{3,1},{4,6},{5,7},{6,4},{7,5},{8,10},{9,11},{10,... | collective-permute-start | bytes 516104 | tf_op jit(solution)/shard_map/ppermute | solution.py:317
  13.1 1.8 %shard_map.103.keep_ref = f32[4,320,128]{2,1,0:T(8,128)S(1)} custom-call(bf16[2,128,5120]{2,1,0:T(8,128)(2,1)} %hidden_ref.7, bf16[2,64,128]{2,1,0:T(8,128)(2,1)} %bitcast.19), custom_call_target="tpu_custom_call" | custom-call | tf_op jit(solution)/shard_map/pallas_call | solution.py:110
  15.0 1.6 %collective-permute-done.2.got_ref = s32[2,168,128]{2,1,0:T(8,128)S(1)} collective-permute-done((s32[2,168,128]{2,1,0:T(8,128)S(1)}, s32[2,168,128]{2,1,0:T(8,128)S(1)}, u32[]{:S(2)}, u32[]{:S(2)}) %collective-permute-start.2) | collective-permute-done | bytes 172064 | tf_op jit(solution)/shard_map/ppermute | solution.py:317
  16.9 2.1 %collective-permute-start.3 = (s32[2,168,128]{2,1,0:T(8,128)S(1)}, s32[2,168,128]{2,1,0:T(8,128)S(1)}, u32[]{:S(2)}, u32[]{:S(2)}) collective-permute-start(s32[2,168,128]{2,1,0:T(8,128)S(1)} %get-tuple-element.19), channel_id=1, source_target_pairs={{0,2},{1,3},{2,0},{3,1},{4,6},{5,7},{6,4},{7,5},{8,10},{9,11},{10,... | collective-permute-start | bytes 516104 | tf_op jit(solution)/shard_map/ppermute | solution.py:317
  19.0 1.6 %collective-permute-start.4 = (s32[1,168,128]{2,1,0:T(8,128)S(1)}, s32[1,168,128]{2,1,0:T(8,128)S(1)}, u32[]{:S(2)}, u32[]{:S(2)}) collective-permute-start(s32[1,168,128]{2,1,0:T(8,128)S(1)} %get-tuple-element.18.refs_0_), channel_id=1, source_target_pairs={{0,4},{1,5},{2,6},{3,7},{4,0},{5,1},{6,2},{7,3},{8,12},{9,13},{10,... | collective-permute-start | bytes 258056 | tf_op jit(solution)/shard_map/ppermute | solution.py:317
  20.5 2.9 %collective-permute-done.4.got_ref = s32[1,168,128]{2,1,0:T(8,128)S(1)} collective-permute-done((s32[1,168,128]{2,1,0:T(8,128)S(1)}, s32[1,168,128]{2,1,0:T(8,128)S(1)}, u32[]{:S(2)}, u32[]{:S(2)}) %collective-permute-start.4) | collective-permute-done | bytes 86048 | tf_op jit(solution)/shard_map/ppermute | solution.py:317
  23.5 2.7 %collective-permute-start.6 = (s32[1,168,128]{2,1,0:T(8,128)S(1)}, s32[1,168,128]{2,1,0:T(8,128)S(1)}, u32[]{:S(2)}, u32[]{:S(2)}) collective-permute-start(s32[1,168,128]{2,1,0:T(8,128)S(1)} %shard_map.109.refs_0_), channel_id=1, source_target_pairs={{0,8},{1,9},{2,10},{3,11},{4,12},{5,13},{6,14},{7,15},{8,0},{9,1},... | collective-permute-start | bytes 258056 | tf_op jit(solution)/shard_map/ppermute | solution.py:317
  26.3 1.6 %collective-permute-start.5 = (s32[1,168,128]{2,1,0:T(8,128)S(1)}, s32[1,168,128]{2,1,0:T(8,128)S(1)}, u32[]{:S(2)}, u32[]{:S(2)}) collective-permute-start(s32[1,168,128]{2,1,0:T(8,128)S(1)} %get-tuple-element.22), channel_id=1, source_target_pairs={{0,4},{1,5},{2,6},{3,7},{4,0},{5,1},{6,2},{7,3},{8,12},{9,13},{10,... | collective-permute-start | bytes 258056 | tf_op jit(solution)/shard_map/ppermute | solution.py:317
  27.9 1.1 %collective-permute-done.6.across_ref = s32[1,168,128]{2,1,0:T(8,128)S(1)} collective-permute-done((s32[1,168,128]{2,1,0:T(8,128)S(1)}, s32[1,168,128]{2,1,0:T(8,128)S(1)}, u32[]{:S(2)}, u32[]{:S(2)}) %collective-permute-start.6) | collective-permute-done | bytes 86048 | tf_op jit(solution)/shard_map/ppermute | solution.py:317
  29.1 1.8 %collective-permute-done.5.got_ref = s32[1,168,128]{2,1,0:T(8,128)S(1)} collective-permute-done((s32[1,168,128]{2,1,0:T(8,128)S(1)}, s32[1,168,128]{2,1,0:T(8,128)S(1)}, u32[]{:S(2)}, u32[]{:S(2)}) %collective-permute-start.5) | collective-permute-done | bytes 86048 | tf_op jit(solution)/shard_map/ppermute | solution.py:317
  31.0 1.4 %collective-permute-done.7.refs_1_ = f32[320,128]{1,0:T(8,128)S(1)} collective-permute-done((f32[320,128]{1,0:T(8,128)S(1)}, f32[320,128]{1,0:T(8,128)S(1)}, u32[]{:S(2)}, u32[]{:S(2)}) %collective-permute-start.7) | collective-permute-done | bytes 163872 | tf_op jit(solution)/shard_map/ppermute | solution.py:317
  32.5 0.9 %collective-permute-start.8 = (f32[8,128]{1,0:T(8,128)S(1)}, f32[8,128]{1,0:T(8,128)S(1)}, u32[]{:S(2)}, u32[]{:S(2)}) collective-permute-start(f32[8,128]{1,0:T(8,128)S(1)} %shard_map.112), channel_id=1, source_target_pairs={{0,24},{1,25},{2,26},{3,27},{4,28},{5,29},{6,30},{7,31},{8,16},{9,... | collective-permute-start | bytes 12296 | tf_op jit(solution)/shard_map/ppermute | solution.py:317
  33.4 3.1 %collective-permute-done.8 = f32[8,128]{1,0:T(8,128)S(1)} collective-permute-done((f32[8,128]{1,0:T(8,128)S(1)}, f32[8,128]{1,0:T(8,128)S(1)}, u32[]{:S(2)}, u32[]{:S(2)}) %collective-permute-start.8) | collective-permute-done | bytes 4128 | tf_op jit(solution)/shard_map/ppermute | solution.py:317
  36.5 1.3 %collective-permute-start.9 = (f32[8,128]{1,0:T(8,128)S(1)}, f32[8,128]{1,0:T(8,128)S(1)}, u32[]{:S(2)}, u32[]{:S(2)}) collective-permute-start(f32[8,128]{1,0:T(8,128)S(1)} %add.9), channel_id=1, source_target_pairs={{0,20},{1,21},{2,22},{3,23},{4,16},{5,17},{6,18},{7,19},{8,28},{9,... | collective-permute-start | bytes 12296 | tf_op jit(solution)/shard_map/ppermute | solution.py:317
  37.8 1.7 %collective-permute-done.9 = f32[8,128]{1,0:T(8,128)S(1)} collective-permute-done((f32[8,128]{1,0:T(8,128)S(1)}, f32[8,128]{1,0:T(8,128)S(1)}, u32[]{:S(2)}, u32[]{:S(2)}) %collective-permute-start.9) | collective-permute-done | bytes 4128 | tf_op jit(solution)/shard_map/ppermute | solution.py:317
  39.5 1.2 %collective-permute-start.10 = (f32[8,128]{1,0:T(8,128)S(1)}, f32[8,128]{1,0:T(8,128)S(1)}, u32[]{:S(2)}, u32[]{:S(2)}) collective-permute-start(f32[8,128]{1,0:T(8,128)S(1)} %add.10), channel_id=1, source_target_pairs={{0,18},{1,19},{2,16},{3,17},{4,22},{5,23},{6,20},{7,21},{8,26},{9,... | collective-permute-start | bytes 12296 | tf_op jit(solution)/shard_map/ppermute | solution.py:317
  40.7 1.8 %collective-permute-done.10 = f32[8,128]{1,0:T(8,128)S(1)} collective-permute-done((f32[8,128]{1,0:T(8,128)S(1)}, f32[8,128]{1,0:T(8,128)S(1)}, u32[]{:S(2)}, u32[]{:S(2)}) %collective-permute-start.10) | collective-permute-done | bytes 4128 | tf_op jit(solution)/shard_map/ppermute | solution.py:317
  42.6 1.2 %collective-permute-start.11 = (f32[8,128]{1,0:T(8,128)S(1)}, f32[8,128]{1,0:T(8,128)S(1)}, u32[]{:S(2)}, u32[]{:S(2)}) collective-permute-start(f32[8,128]{1,0:T(8,128)S(1)} %add.11.sums_ref), channel_id=1, source_target_pairs={{0,17},{1,16},{2,19},{3,18},{4,21},{5,20},{6,23},{7,22},{8,25},{9,... | collective-permute-start | bytes 12296 | tf_op jit(solution)/shard_map/ppermute | solution.py:317
  45.6 1.2 %shard_map.114 = (f32[64,320]{1,0:T(8,128)}, f32[64,320]{1,0:T(8,128)}, f32[64,320]{1,0:T(8,128)}, f32[1,4]{1,0:T(1,128)}) custom-call(f32[8,128]{1,0:T(8,128)S(1)} %add.11.sums_ref, f32[8,128]{1,0:T(8,128)S(1)} %collective-permute-done.11.got_ref, f32[2,128,320]{2,1,0:T(8,128)S(1)} %shard_map.113.grad_ref, f32[1,4]{1,0:T(1,128)S(1)} %bitcast.13, ...), custom_call_target="tpu_custom_call" | custom-call | tf_op jit(solution)/shard_map/pallas_call | solution.py:299
  (28 shorter events, 2.9 us)
Async XLA Ops:
  2.5 8.3 %collective-permute-start.1 = (s32[4,168,128]{2,1,0:T(8,128)S(1)}, s32[4,168,128]{2,1,0:T(8,128)S(1)}, u32[]{:S(2)}, u32[]{:S(2)}) collective-permute-start(s32[4,168,128]{2,1,0:T(8,128)S(1)} %shard_map.104), channel_id=1, source_target_pairs={{0,1},{1,0},{2,3},{3,2},{4,5},{5,4},{6,7},{7,6},{8,9},{9,8},{10,11... | collective-permute-start | bytes 1032200 | tf_op jit(solution)/shard_map/ppermute | solution.py:317
  7.5 9.2 %collective-permute-start = (s32[4,168,128]{2,1,0:T(8,128)S(1)}, s32[4,168,128]{2,1,0:T(8,128)S(1)}, u32[]{:S(2)}, u32[]{:S(2)}) collective-permute-start(s32[4,168,128]{2,1,0:T(8,128)S(1)} %shard_map.102), channel_id=1, source_target_pairs={{0,1},{1,0},{2,3},{3,2},{4,5},{5,4},{6,7},{7,6},{8,9},{9,8},{10,11... | collective-permute-start | bytes 1032200 | tf_op jit(solution)/shard_map/ppermute | solution.py:317
  11.0 32.8 %copy-start.4 = (s32[2]{0:T(128)S(1)}, s32[2]{0:T(128)}, u32[]{:S(2)}) copy-start(s32[2]{0:T(128)} %param.9) | copy-start | bytes 28
  11.0 5.5 %collective-permute-start.2 = (s32[2,168,128]{2,1,0:T(8,128)S(1)}, s32[2,168,128]{2,1,0:T(8,128)S(1)}, u32[]{:S(2)}, u32[]{:S(2)}) collective-permute-start(s32[2,168,128]{2,1,0:T(8,128)S(1)} %get-tuple-element.16), channel_id=1, source_target_pairs={{0,2},{1,3},{2,0},{3,1},{4,6},{5,7},{6,4},{7,5},{8,10},{9,11},{10,... | collective-permute-start | bytes 516104 | tf_op jit(solution)/shard_map/ppermute | solution.py:317
  14.9 30.7 %copy-start = (f32[320,64]{0,1:T(8,128)S(1)}, f32[320,64]{0,1:T(8,128)}, u32[]{:S(2)}) copy-start(f32[320,64]{0,1:T(8,128)} %param.11) | copy-start | bytes 245764
  14.9 30.7 %copy-start.1 = (f32[320,64]{0,1:T(8,128)S(1)}, f32[320,64]{0,1:T(8,128)}, u32[]{:S(2)}) copy-start(f32[320,64]{0,1:T(8,128)} %param.12) | copy-start | bytes 245764
  14.9 30.7 %copy-start.2 = (f32[320,64]{0,1:T(8,128)S(1)}, f32[320,64]{0,1:T(8,128)}, u32[]{:S(2)}) copy-start(f32[320,64]{0,1:T(8,128)} %param.13) | copy-start | bytes 245764
  14.9 30.7 %copy-start.3 = (f32[4]{0:T(128)S(1)}, f32[4]{0:T(128)}, u32[]{:S(2)}) copy-start(f32[4]{0:T(128)} %param.10) | copy-start | bytes 52
  16.9 9.3 %collective-permute-start.3 = (s32[2,168,128]{2,1,0:T(8,128)S(1)}, s32[2,168,128]{2,1,0:T(8,128)S(1)}, u32[]{:S(2)}, u32[]{:S(2)}) collective-permute-start(s32[2,168,128]{2,1,0:T(8,128)S(1)} %get-tuple-element.19), channel_id=1, source_target_pairs={{0,2},{1,3},{2,0},{3,1},{4,6},{5,7},{6,4},{7,5},{8,10},{9,11},{10,... | collective-permute-start | bytes 516104 | tf_op jit(solution)/shard_map/ppermute | solution.py:317
  19.0 4.5 %collective-permute-start.4 = (s32[1,168,128]{2,1,0:T(8,128)S(1)}, s32[1,168,128]{2,1,0:T(8,128)S(1)}, u32[]{:S(2)}, u32[]{:S(2)}) collective-permute-start(s32[1,168,128]{2,1,0:T(8,128)S(1)} %get-tuple-element.18.refs_0_), channel_id=1, source_target_pairs={{0,4},{1,5},{2,6},{3,7},{4,0},{5,1},{6,2},{7,3},{8,12},{9,13},{10,... | collective-permute-start | bytes 258056 | tf_op jit(solution)/shard_map/ppermute | solution.py:317
  23.5 5.5 %collective-permute-start.6 = (s32[1,168,128]{2,1,0:T(8,128)S(1)}, s32[1,168,128]{2,1,0:T(8,128)S(1)}, u32[]{:S(2)}, u32[]{:S(2)}) collective-permute-start(s32[1,168,128]{2,1,0:T(8,128)S(1)} %shard_map.109.refs_0_), channel_id=1, source_target_pairs={{0,8},{1,9},{2,10},{3,11},{4,12},{5,13},{6,14},{7,15},{8,0},{9,1},... | collective-permute-start | bytes 258056 | tf_op jit(solution)/shard_map/ppermute | solution.py:317
  26.3 4.6 %collective-permute-start.5 = (s32[1,168,128]{2,1,0:T(8,128)S(1)}, s32[1,168,128]{2,1,0:T(8,128)S(1)}, u32[]{:S(2)}, u32[]{:S(2)}) collective-permute-start(s32[1,168,128]{2,1,0:T(8,128)S(1)} %get-tuple-element.22), channel_id=1, source_target_pairs={{0,4},{1,5},{2,6},{3,7},{4,0},{5,1},{6,2},{7,3},{8,12},{9,13},{10,... | collective-permute-start | bytes 258056 | tf_op jit(solution)/shard_map/ppermute | solution.py:317
  30.9 1.5 %collective-permute-start.7 = (f32[320,128]{1,0:T(8,128)S(1)}, f32[320,128]{1,0:T(8,128)S(1)}, u32[]{:S(2)}, u32[]{:S(2)}) collective-permute-start(f32[320,128]{1,0:T(8,128)S(1)} %shard_map.111.refs_0_), channel_id=1, source_target_pairs={{0,16},{1,17},{2,18},{3,19},{4,20},{5,21},{6,22},{7,23},{8,24},{9,... | collective-permute-start | bytes 491528 | tf_op jit(solution)/shard_map/ppermute | solution.py:317
  32.5 4.0 %collective-permute-start.8 = (f32[8,128]{1,0:T(8,128)S(1)}, f32[8,128]{1,0:T(8,128)S(1)}, u32[]{:S(2)}, u32[]{:S(2)}) collective-permute-start(f32[8,128]{1,0:T(8,128)S(1)} %shard_map.112), channel_id=1, source_target_pairs={{0,24},{1,25},{2,26},{3,27},{4,28},{5,29},{6,30},{7,31},{8,16},{9,... | collective-permute-start | bytes 12296 | tf_op jit(solution)/shard_map/ppermute | solution.py:317
  36.5 3.0 %collective-permute-start.9 = (f32[8,128]{1,0:T(8,128)S(1)}, f32[8,128]{1,0:T(8,128)S(1)}, u32[]{:S(2)}, u32[]{:S(2)}) collective-permute-start(f32[8,128]{1,0:T(8,128)S(1)} %add.9), channel_id=1, source_target_pairs={{0,20},{1,21},{2,22},{3,23},{4,16},{5,17},{6,18},{7,19},{8,28},{9,... | collective-permute-start | bytes 12296 | tf_op jit(solution)/shard_map/ppermute | solution.py:317
  39.5 3.0 %collective-permute-start.10 = (f32[8,128]{1,0:T(8,128)S(1)}, f32[8,128]{1,0:T(8,128)S(1)}, u32[]{:S(2)}, u32[]{:S(2)}) collective-permute-start(f32[8,128]{1,0:T(8,128)S(1)} %add.10), channel_id=1, source_target_pairs={{0,18},{1,19},{2,16},{3,17},{4,22},{5,23},{6,20},{7,21},{8,26},{9,... | collective-permute-start | bytes 12296 | tf_op jit(solution)/shard_map/ppermute | solution.py:317
  42.6 3.0 %collective-permute-start.11 = (f32[8,128]{1,0:T(8,128)S(1)}, f32[8,128]{1,0:T(8,128)S(1)}, u32[]{:S(2)}, u32[]{:S(2)}) collective-permute-start(f32[8,128]{1,0:T(8,128)S(1)} %add.11.sums_ref), channel_id=1, source_target_pairs={{0,17},{1,16},{2,19},{3,18},{4,21},{5,20},{6,23},{7,22},{8,25},{9,... | collective-permute-start | bytes 12296 | tf_op jit(solution)/shard_map/ppermute | solution.py:317
  43.8 1.2 %collective-permute-start.12 = (s32[1,2]{1,0:T(1,128)S(1)}, s32[1,2]{1,0:T(1,128)S(1)}, u32[]{:S(2)}, u32[]{:S(2)}) collective-permute-start(s32[1,2]{1,0:T(1,128)S(1)} %bitcast.14), channel_id=1, source_target_pairs={{0,16},{1,17},{2,18},{3,19},{4,20},{5,21},{6,22},{7,23},{8,24},{9,... | collective-permute-start | bytes 32 | tf_op jit(solution)/shard_map/ppermute | solution.py:317
